TPU v7x, 128 devices: a whole 4x4x4 slice. The times are simulated.
128 devices in a mesh: chan: 4 (over z), rows: 32 (over y, x, core).
Axes of the slice: x: 4, y: 4, z: 4, core: 2. Of those that a mesh axis runs over, the one named last changes fastest.
Arguments:
- estimate: float32 [4, 2048, 2048], P('chan', 'rows'), may hold values from -3 to 3
- dirty_image: float32 [4, 2048, 2048], P('chan', 'rows'), may hold values from -40 to 40
- psf_weights: float32 [4, 2048, 2048], P('chan', None, 'rows'), may hold values from 0.05 to 2
Outputs:
- new_estimate: float32 [4, 2048, 2048], P('chan', 'rows')
- residual: float32 [4, 2048, 2048], P('chan', 'rows')
All inputs are finite; a program needn't handle non-finite values.
Results may differ from a plain program's by a relative error of at most 0.0001.
Values sent between devices are 32-bit elements; how exact they have to be, the bound alone decides.
A program may use at most 64 MiB of HBM per device.

v0:
```python
import functools
import math

import jax
import jax.numpy as jnp
import numpy as np
from jax import lax
from jax.experimental import pallas as pl
from jax.experimental.pallas import tpu as pltpu
from jax.sharding import PartitionSpec as P

fractions = (0.03, 0.02, 0.015)
step_size = 0.9
MESH = pl.DeviceIdType.MESH
F32 = jnp.float32
BF16 = jnp.bfloat16
R = 32
Z = 4
TILES = 5


def linear(pairs):
    total = None
    for coef, value in pairs:
        if abs(coef) < 1e-12:
            continue
        if abs(coef - 1.0) < 1e-12:
            total = value if total is None else total + value
        elif abs(coef + 1.0) < 1e-12:
            total = -value if total is None else total - value
        else:
            term = coef * value
            total = term if total is None else total + term
    return total


def cosine_16(first, middle, e):
    out = [None] * 9
    for k in range(5):
        even = linear(
            [(1.0, first), (1.0 if k % 2 == 0 else -1.0, middle)]
            + [(math.cos(2 * math.pi * k * a / 16), e[a]) for a in (2, 4, 6)]
        )
        odd = linear([(math.cos(2 * math.pi * k * a / 16), e[a]) for a in (1, 3, 5, 7)])
        if odd is None:
            out[k] = even
            out[8 - k] = even
        else:
            out[k] = even + odd
            out[8 - k] = even - odd
    return out


def sine_16(o):
    out = [None] * 8
    for k in range(1, 5):
        even = linear([(math.sin(2 * math.pi * k * a / 16), o[a]) for a in (2, 4, 6)])
        odd = linear([(math.sin(2 * math.pi * k * a / 16), o[a]) for a in (1, 3, 5, 7)])
        if even is None:
            out[k] = odd
        else:
            out[k] = odd + even
            out[8 - k] = odd - even
    return out


def fft(values, sign):
    count = len(values)
    if count == 1:
        return values
    if count == 2:
        (ar, ai), (br, bi) = values
        return [(ar + br, ai + bi), (ar - br, ai - bi)]
    if count == 4:
        (ar, ai), (br, bi), (cr, ci), (dr, di) = values
        sr, si, tr, ti = ar + cr, ai + ci, ar - cr, ai - ci
        ur, ui, vr, vi = br + dr, bi + di, br - dr, bi - di
        if sign > 0:
            return [(sr + ur, si + ui), (tr - vi, ti + vr), (sr - ur, si - ui), (tr + vi, ti - vr)]
        return [(sr + ur, si + ui), (tr + vi, ti - vr), (sr - ur, si - ui), (tr - vi, ti + vr)]
    quarter = count // 4
    parts = [fft(values[n::4], sign) for n in range(4)]
    out = [None] * count
    for k in range(quarter):
        four = []
        for n in range(4):
            re, im = parts[n][k]
            angle = sign * 2 * math.pi * n * k / count
            c, s = math.cos(angle), math.sin(angle)
            if n * k == 0:
                four.append((re, im))
            elif abs(abs(c) - abs(s)) < 1e-9:
                h = abs(c)
                cs, ss = math.copysign(1, c), math.copysign(1, s)
                r = (re if cs > 0 else -re) - (im if ss > 0 else -im)
                i = (im if cs > 0 else -im) + (re if ss > 0 else -re)
                four.append((h * r, h * i))
            else:
                four.append((re * c - im * s, re * s + im * c))
        for m, value in enumerate(fft(four, sign)):
            out[k + m * quarter] = value
    return out


def split(value):
    high = value.astype(BF16)
    return high, (value - high.astype(F32)).astype(BF16)


def dot3(a, b, dims):
    (ah, al), (bh, bl) = a, b
    dot = functools.partial(
        lax.dot_general, dimension_numbers=(dims, ((), ())), preferred_element_type=F32
    )
    return dot(ah, bh) + (dot(al, bh) + dot(ah, bl))


def tables():
    m = np.arange(128)
    rows = np.zeros((256, 256))
    for d in range(32):
        for jj in range(4):
            angle = 2 * np.pi * ((4 * d + jj) * m % 128) / 128
            rows[8 * d + jj] = np.concatenate([np.cos(angle), np.sin(angle)])
            rows[8 * d + 4 + jj] = np.concatenate([-np.sin(angle), np.cos(angle)])
    n = np.arange(64)
    angle = 2 * np.pi * (n[:, None] * n[None, :] % 64) / 64
    cols = np.zeros((2, 2, 64, 2, 2, 64))
    for kk in range(2):
        cols[0, kk, :, 0, kk] = np.cos(angle)
        cols[1, kk, :, 0, kk] = np.sin(angle)
        cols[0, kk, :, 1, kk] = -np.sin(angle)
        cols[1, kk, :, 1, kk] = np.cos(angle)
    cols = cols.reshape(256, 256)
    k = np.arange(1, 9)
    angle = -2 * np.pi * k[:, None] * m[None, :] / 2048
    row_twist = np.concatenate([np.cos(angle), np.sin(angle)])
    u1 = np.arange(32)
    angle = -2 * np.pi * u1[:, None] * n[None, :] / 2048
    angle = np.concatenate([angle, angle], axis=1)
    col_twist = np.stack([np.cos(angle), np.sin(angle)])

    def halves(table):
        high = table.astype(BF16)
        return np.stack([high, (table - high.astype(np.float64)).astype(BF16)])

    return (
        halves(rows),
        halves(cols),
        halves(cols.T),
        np.asarray(row_twist, np.float32),
        np.asarray(col_twist, np.float32),
    )


def roll(value, shift, axis):
    return pltpu.roll(value, shift % value.shape[axis], axis)


def smooth(value, spacing):
    for axis in (1, 0):
        value = value + roll(value, spacing, axis)
        value = value + roll(value, -spacing, axis)
        value = value + roll(value, spacing, axis)
        value = value + roll(value, -spacing, axis)
    return value * (1.0 / 256.0)


def kernel(
    est, dirty, weights, row_table, col_table, col_back, row_twist, col_twist,
    new_ref, res_ref,
    abuf, send, recv, spec, send2, recv2, hz, hr, det, energy, ob, mx_own, mx_z, mx_r,
    s_send, s_recv, s_send2, s_recv2, z_send, z_recv, h_send, h_recv, o_send, o_recv,
    mz_send, mz_recv, mr_send, mr_recv, own_sem,
):
    z = lax.axis_index("chan")
    p = lax.axis_index("rows")

    barrier = pltpu.get_barrier_semaphore()

    def greet_row(i, carry):
        pl.semaphore_signal(
            barrier, inc=1, device_id={"rows": lax.rem(p + i, R)}, device_id_type=MESH
        )
        return carry

    def greet_chan(i, carry):
        pl.semaphore_signal(
            barrier, inc=1, device_id={"chan": lax.rem(z + i, Z)}, device_id_type=MESH
        )
        return carry

    lax.fori_loop(1, R, greet_row, 0)
    lax.fori_loop(1, Z, greet_chan, 0)

    abuf[576:640, :] = jnp.zeros((64, 256), F32)

    def rows_forward(g, carry):
        at = pl.ds(pl.multiple_of(8 * g, 8), 8)
        x = [est[at, 128 * a : 128 * a + 128] for a in range(16)]
        e = [None] + [x[a] + x[16 - a] for a in range(1, 8)]
        o = [None] + [x[a] - x[16 - a] for a in range(1, 8)]
        re = cosine_16(x[0], x[8], e)
        im = sine_16(o)
        for k in range(1, 9):
            c = row_twist[k - 1 : k, :]
            s = row_twist[k + 7 : k + 8, :]
            to = pl.ds(pl.multiple_of(64 * (k - 1) + 8 * g, 8), 8)
            if k < 8:
                abuf[to, 0:128] = re[k] * c + im[k] * s
                abuf[to, 128:256] = re[k] * s - im[k] * c
            else:
                abuf[to, 0:128] = re[k] * c
                abuf[to, 128:256] = re[k] * s
        to = pl.ds(pl.multiple_of(512 + 8 * g, 8), 8)
        abuf[to, 0:128] = re[0]
        abuf[to, 128:256] = jnp.zeros((8, 128), F32)
        return carry

    lax.fori_loop(0, 8, rows_forward, 0)
    table = (row_table[0], row_table[1])
    for t in range(TILES):
        out = dot3(table, split(abuf[128 * t : 128 * t + 128, :]), ((1,), (1,)))
        send[:, t] = out.reshape(R, 8, 128)

    pl.semaphore_wait(barrier, R - 1 + Z - 1)

    def exchange(source, target, send_sem, recv_sem):
        def copy(to, slot, sem):
            return pltpu.make_async_remote_copy(
                src_ref=source.at[to],
                dst_ref=target.at[slot, 0:TILES],
                send_sem=send_sem.at[to],
                recv_sem=recv_sem.at[sem],
                device_id={"rows": to},
                device_id_type=MESH,
            )

        def begin(i, carry):
            copy(lax.rem(p + i, R), p, p).start()
            return carry

        lax.fori_loop(1, R, begin, 0)
        own = pltpu.make_async_copy(source.at[p], target.at[p, 0:TILES], own_sem)
        own.start()

        def end(i, carry):
            other = lax.rem(p + R - i, R)
            copy(other, other, other).wait_recv()
            return carry

        lax.fori_loop(1, R, end, 0)
        own.wait()

        def sent(i, carry):
            to = lax.rem(p + i, R)
            copy(to, p, p).wait_send()
            return carry

        lax.fori_loop(1, R, sent, 0)

    exchange(send, recv, s_send, s_recv)

    recv[:, TILES] = jnp.zeros((R, 8, 128), F32)
    upper = lax.broadcasted_iota(jnp.int32, (8, 128), 0) < 4

    def columns(q, carry):
        values = []
        for i in range(R):
            a = recv[i, 2 * q]
            b = recv[i, 2 * q + 1]
            values.append(
                (jnp.where(upper, a, roll(b, 4, 0)), jnp.where(upper, roll(a, 4, 0), b))
            )
        for u, (re, im) in enumerate(fft(values, -1)):
            c = col_twist[0, u : u + 1, :]
            s = col_twist[1, u : u + 1, :]
            spec[8 * u : 8 * u + 8, 0:128] = re * c - im * s
            spec[8 * u : 8 * u + 8, 128:256] = re * s + im * c
        out = dot3(split(spec[...]), (col_table[0], col_table[1]), ((1,), (0,)))
        w = weights[q].reshape(256, 128)
        out = jnp.concatenate([out[:, 0:128] * w, out[:, 128:256] * w], axis=1)
        spec[...] = dot3(split(out), (col_back[0], col_back[1]), ((1,), (0,)))
        values = []
        for u in range(R):
            c = col_twist[0, u : u + 1, :]
            s = col_twist[1, u : u + 1, :]
            re = spec[8 * u : 8 * u + 8, 0:128]
            im = spec[8 * u : 8 * u + 8, 128:256]
            values.append((re * c + im * s, im * c - re * s))
        for i, (re, im) in enumerate(fft(values, 1)):
            send2[i, 2 * q] = jnp.where(upper, re, roll(im, 4, 0))
            send2[i, 2 * q + 1] = jnp.where(upper, roll(re, 4, 0), im)
        return carry

    lax.fori_loop(0, 3, columns, 0)

    def copy2(to, slot, sem):
        return pltpu.make_async_remote_copy(
            src_ref=send2.at[to, 0:TILES],
            dst_ref=recv2.at[slot],
            send_sem=s_send2.at[to],
            recv_sem=s_recv2.at[sem],
            device_id={"rows": to},
            device_id_type=MESH,
        )

    def begin2(i, carry):
        copy2(lax.rem(p + i, R), p, p).start()
        return carry

    lax.fori_loop(1, R, begin2, 0)
    own2 = pltpu.make_async_copy(send2.at[p, 0:TILES], recv2.at[p], own_sem)
    own2.start()

    def end2(i, carry):
        other = lax.rem(p + R - i, R)
        copy2(other, other, other).wait_recv()
        return carry

    lax.fori_loop(1, R, end2, 0)
    own2.wait()

    for t in range(TILES):
        block = recv2[:, t].reshape(256, 128)
        abuf[128 * t : 128 * t + 128, :] = dot3(split(block), table, ((0,), (0,)))

    for c in range(Z):
        if c == 0:
            hz[c, :, 0:128] = jnp.zeros((64, 128), F32)
        if c == Z - 1:
            hz[c, :, 640:768] = jnp.zeros((64, 128), F32)

    def rows_inverse(g, carry):
        re, im = [None] * 9, [None] * 8
        for k in range(1, 9):
            c = row_twist[k - 1 : k, :]
            s = row_twist[k + 7 : k + 8, :]
            to = pl.ds(pl.multiple_of(64 * (k - 1) + 8 * g, 8), 8)
            gr, gi = abuf[to, 0:128], abuf[to, 128:256]
            re[k] = gr * c + gi * s
            if k < 8:
                im[k] = gi * c - gr * s
        re[0] = abuf[pl.ds(pl.multiple_of(512 + 8 * g, 8), 8), 0:128]
        cosine = cosine_16(re[0], re[8], re)
        sine = sine_16(im)
        at = pl.ds(pl.multiple_of(8 * g, 8), 8)
        for a in range(16):
            if a == 0 or a == 8:
                blurred = cosine[a]
            elif a < 8:
                blurred = cosine[a] - sine[a]
            else:
                blurred = cosine[16 - a] + sine[16 - a]
            lanes = slice(128 * a, 128 * a + 128)
            residual = dirty[at, lanes] - blurred
            res_ref[at, lanes] = residual
            halfway = est[at, lanes] + step_size * residual
            own = a // 4
            hz[own, at, 128 * (a % 4) + 128 : 128 * (a % 4) + 256] = halfway
            if a % 4 == 0 and own > 0:
                hz[own - 1, at, 640:768] = halfway
            if a % 4 == 3 and own < Z - 1:
                hz[own + 1, at, 0:128] = halfway
        return carry

    lax.fori_loop(0, 8, rows_inverse, 0)

    def copy_z(to, slot, sem):
        return pltpu.make_async_remote_copy(
            src_ref=hz.at[to],
            dst_ref=hr.at[slot, 16:80, :],
            send_sem=z_send.at[to],
            recv_sem=z_recv.at[sem],
            device_id={"chan": to},
            device_id_type=MESH,
        )

    for i in range(1, Z):
        copy_z(lax.rem(z + i, Z), z, z).start()
    own3 = pltpu.make_async_copy(hz.at[z], hr.at[z, 16:80, :], own_sem)
    own3.start()

    @pl.when(p == 0)
    def _():
        hr[:, 0:16, :] = jnp.zeros((Z, 16, 768), F32)

    @pl.when(p == R - 1)
    def _():
        hr[:, 80:96, :] = jnp.zeros((Z, 16, 768), F32)

    for i in range(1, Z):
        other = lax.rem(z + Z - i, Z)
        copy_z(other, other, other).wait_recv()
    own3.wait()

    above = pltpu.make_async_remote_copy(
        src_ref=hr.at[:, 16:32, :],
        dst_ref=hr.at[:, 80:96, :],
        send_sem=h_send.at[0],
        recv_sem=h_recv.at[0],
        device_id={"rows": lax.rem(p + R - 1, R)},
        device_id_type=MESH,
    )
    below = pltpu.make_async_remote_copy(
        src_ref=hr.at[:, 64:80, :],
        dst_ref=hr.at[:, 0:16, :],
        send_sem=h_send.at[1],
        recv_sem=h_recv.at[1],
        device_id={"rows": lax.rem(p + 1, R)},
        device_id_type=MESH,
    )

    @pl.when(p > 0)
    def _():
        above.start()

    @pl.when(p < R - 1)
    def _():
        below.start()

    @pl.when(p < R - 1)
    def _():
        above.wait_recv()

    @pl.when(p > 0)
    def _():
        below.wait_recv()

    row_ids = lax.broadcasted_iota(jnp.int32, (96, 1), 0) + 64 * p - 16
    col_ids = lax.broadcasted_iota(jnp.int32, (1, 768), 1) + 512 * z - 128
    row_mask = jnp.logical_and(row_ids >= 0, row_ids < 64 * R).astype(F32)
    col_mask = jnp.logical_and(col_ids >= 0, col_ids < 512 * Z).astype(F32)

    def starlet(ch, carry):
        current = hr[ch]
        for level in range(3):
            later = smooth(current, 1 << level)
            if level < 2:
                later = later * row_mask * col_mask
            detail = (current - later)[16:80, 128:640]
            det[level, ch] = detail
            squared = detail * detail
            energy[level] = jnp.where(ch == 0, squared, energy[level] + squared)
            current = later
        return carry

    energy[...] = jnp.zeros((3, 64, 512), F32)
    lax.fori_loop(0, Z, starlet, 0)

    lane = lax.broadcasted_iota(jnp.int32, (1, 128), 1)
    peaks = jnp.zeros((1, 128), F32)
    for level in range(3):
        peaks = jnp.where(lane == level, jnp.max(energy[level]), peaks)
    mx_own[0] = peaks

    def copy_mz(to, slot):
        return pltpu.make_async_remote_copy(
            src_ref=mx_own.at[0],
            dst_ref=mx_z.at[slot],
            send_sem=mz_send.at[to],
            recv_sem=mz_recv.at[slot],
            device_id={"chan": to},
            device_id_type=MESH,
        )

    for i in range(1, Z):
        copy_mz(lax.rem(z + i, Z), z).start()
    mx_z[z] = peaks
    for i in range(1, Z):
        other = lax.rem(z + Z - i, Z)
        copy_mz(other, other).wait_recv()
    peaks = jnp.max(mx_z[...], axis=0)
    mx_own[1] = peaks

    def copy_mr(to, slot):
        return pltpu.make_async_remote_copy(
            src_ref=mx_own.at[1],
            dst_ref=mx_r.at[slot],
            send_sem=mr_send.at[to],
            recv_sem=mr_recv.at[slot],
            device_id={"rows": to},
            device_id_type=MESH,
        )

    def begin_mr(i, carry):
        copy_mr(lax.rem(p + i, R), p).start()
        return carry

    lax.fori_loop(1, R, begin_mr, 0)
    mx_r[p] = peaks
    energy[...] = lax.rsqrt(energy[...])

    def end_mr(i, carry):
        other = lax.rem(p + R - i, R)
        copy_mr(other, other).wait_recv()
        return carry

    lax.fori_loop(1, R, end_mr, 0)
    peaks = jnp.sqrt(jnp.max(mx_r[...], axis=0))
    thresholds = [
        fractions[level] * jnp.max(jnp.where(lane == level, peaks, 0.0)) for level in range(3)
    ]
    for level in range(3):
        energy[level] = jnp.minimum(energy[level] * thresholds[level], 1.0)

    def copy_o(to, slot, sem):
        return pltpu.make_async_remote_copy(
            src_ref=ob.at[to],
            dst_ref=new_ref.at[:, pl.ds(pl.multiple_of(512 * slot, 512), 512)],
            send_sem=o_send.at[to],
            recv_sem=o_recv.at[sem],
            device_id={"chan": to},
            device_id_type=MESH,
        )

    def final(i, carry):
        ch = lax.rem(z + i, Z)
        out = hr[ch, 16:80, 128:640]
        for level in range(3):
            out = out - energy[level] * det[level, ch]
        ob[ch] = out
        copy_o(ch, z, z).start()
        return carry

    lax.fori_loop(1, Z, final, 0)
    out = hr[z, 16:80, 128:640]
    for level in range(3):
        out = out - energy[level] * det[level, z]
    new_ref[:, pl.ds(pl.multiple_of(512 * z, 512), 512)] = out

    def sent2(i, carry):
        to = lax.rem(p + i, R)
        copy2(to, p, p).wait_send()
        copy_mr(to, p).wait_send()
        return carry

    lax.fori_loop(1, R, sent2, 0)

    @pl.when(p > 0)
    def _():
        above.wait_send()

    @pl.when(p < R - 1)
    def _():
        below.wait_send()

    for i in range(1, Z):
        other = lax.rem(z + Z - i, Z)
        copy_o(other, other, other).wait_recv()
    for i in range(1, Z):
        to = lax.rem(z + i, Z)
        copy_z(to, z, z).wait_send()
        copy_mz(to, z).wait_send()
        copy_o(to, z, z).wait_send()


def arrange_weights(w):
    other = lax.ppermute(w, "rows", [(i, R - 1 - i) for i in range(R)])
    mirror = jnp.roll(jnp.flip(other, axis=0), 1, axis=0)
    mirror = jnp.roll(jnp.flip(mirror, axis=1), 1, axis=1)
    w4 = w.reshape(64, 32, 4, 16)
    m4 = mirror.reshape(64, 32, 4, 16)
    both = jnp.concatenate(
        [
            w4[..., 1:8] + m4[..., 1:8],
            w4[..., 8:9],
            w4[..., 0:1],
            jnp.zeros((64, 32, 4, 3), F32),
        ],
        axis=3,
    ) * (1.0 / (2048.0 * 2048.0))
    both = both.reshape(64, 32, 4, 3, 2, 2)
    return both.transpose(3, 1, 4, 2, 5, 0).reshape(3, 32, 8, 128)


def shards(estimate, dirty_image, psf_weights):
    weights = arrange_weights(psf_weights[0])
    constants = tables()
    vmem = pl.BlockSpec(memory_space=pltpu.VMEM)
    block = jax.ShapeDtypeStruct((64, 2048), F32)
    dma = pltpu.SemaphoreType.DMA
    new, res = pl.pallas_call(
        kernel,
        out_shape=(block, block),
        in_specs=[vmem] * 8,
        out_specs=(vmem, vmem),
        scratch_shapes=[
            pltpu.VMEM((640, 256), F32),
            pltpu.VMEM((R, TILES, 8, 128), F32),
            pltpu.VMEM((R, TILES + 1, 8, 128), F32),
            pltpu.VMEM((256, 256), F32),
            pltpu.VMEM((R, TILES + 1, 8, 128), F32),
            pltpu.VMEM((R, TILES, 8, 128), F32),
            pltpu.VMEM((Z, 64, 768), F32),
            pltpu.VMEM((Z, 96, 768), F32),
            pltpu.VMEM((3, Z, 64, 512), F32),
            pltpu.VMEM((3, 64, 512), F32),
            pltpu.VMEM((Z, 64, 512), F32),
            pltpu.VMEM((2, 1, 128), F32),
            pltpu.VMEM((Z, 1, 128), F32),
            pltpu.VMEM((R, 1, 128), F32),
            dma((R,)), dma((R,)), dma((R,)), dma((R,)),
            dma((Z,)), dma((Z,)), dma((2,)), dma((2,)), dma((Z,)), dma((Z,)),
            dma((Z,)), dma((Z,)), dma((R,)), dma((R,)), dma,
        ],
        compiler_params=pltpu.CompilerParams(collective_id=0, has_side_effects=True),
    )(estimate[0], dirty_image[0], weights, *constants)
    return (new[None], res[None])


def solution(mesh):
    return jax.shard_map(
        shards,
        mesh=mesh,
        in_specs=(P("chan", "rows", None), P("chan", "rows", None), P("chan", None, "rows")),
        out_specs=(P("chan", "rows", None), P("chan", "rows", None)),
        check_vma=False,
    )
```

profile of v0, /device:TPU:1, one launch (start us, length us, event | category | flops | bytes accessed | tf_op | source)
XLA Modules:
  0.0 104.4 jit_solution(15018169439471348316)
XLA Ops:
  0.6 6.4 %collective-permute-start = (f32[2048,64]{0,1:T(8,128)}, f32[2048,64]{0,1:T(8,128)}, u32[]{:S(2)}, u32[]{:S(2)}) collective-permute-start(f32[2048,64]{0,1:T(8,128)} %bitcast.15), channel_id=1, source_target_pairs={{0,31},{1,30},{2,29},{3,28},{4,27},{5,26},{6,25},{7,24},{8,23},{9,... | collective-permute-start | bytes 1572872 | tf_op jit(solution)/shard_map/ppermute | solution.py:559
  7.0 1.8 %reshape_squeeze.3 = f32[64,32,4,16]{1,0,3,2:T(8,128)S(1)} reshape(f32[1,2048,64]{1,2,0:T(8,128)} %param.10) | data formatting | bytes 1048576 | tf_op jit(solution)/shard_map/reshape;squeeze | solution.py:562
  8.8 0.1 slice.46
  9.0 0.1 copy.20
  9.0 0.7 copy.19
  9.8 0.3 copy.17
  10.1 9.1 %collective-permute-done = f32[2048,64]{0,1:T(8,128)} collective-permute-done((f32[2048,64]{0,1:T(8,128)}, f32[2048,64]{0,1:T(8,128)}, u32[]{:S(2)}, u32[]{:S(2)}) %collective-permute-start) | collective-permute-done | bytes 524320 | tf_op jit(solution)/shard_map/ppermute | solution.py:559
  19.3 1.2 %slice.48 = f32[2047,64]{0,1:T(8,128)S(1)} slice(f32[2048,64]{0,1:T(8,128)} %collective-permute-done), slice={[1:2048], [0:64]} | slice | bytes 1048064 | tf_op jit(solution)/shard_map/jit(_roll_static)/slice | solution.py:560
  20.5 1.3 %reverse.4 = f32[2048,64]{0,1:T(8,128)S(1)} reverse(f32[2048,64]{0,1:T(8,128)S(1)} %bitcast.14), dimensions={0} | reverse | bytes 1048576
  21.8 0.2 slice.52
  22.0 0.8 slice.47
  22.8 0.2 pad_maximum_fusion
  23.0 0.5 slice.42
  23.5 0.1 fusion
  23.6 0.7 reshape.14
  24.3 0.1 slice.49
  24.4 0.3 copy.18
  24.8 0.5 copy-done
  25.2 0.1 maximum_multiply_fusion
  25.4 0.6 copy.16
  26.0 1.2 %reshape.15.weights = f32[3,32,8,128]{3,2,1,0:T(8,128)} reshape(f32[3,32,2,4,2,64]{5,4,3,2,1,0:T(2,128)S(1)} %copy.16) | data formatting | bytes 786432 | tf_op jit(solution)/shard_map/reshape | solution.py:574
  27.2 73.5 %shard_map.95 = (f32[64,2048]{1,0:T(8,128)}, f32[64,2048]{1,0:T(8,128)}) custom-call(f32[64,2048]{1,0:T(8,128)} %bitcast.16, f32[64,2048]{1,0:T(8,128)} %bitcast.17, f32[3,32,8,128]{3,2,1,0:T(8,128)} %reshape.15.weights, bf16[2,256,256]{2,1,0:T(8,128)(2,1)} %constant.14.clone.row_table, bf16[2,256,256]{2,1,0:T(8,128)(2,1)} %constant.15.clone.col_table, ...), custom_call_target="tpu_custom_call" | custom-call | tf_op jit(solution)/shard_map/pallas_call | solution.py:583
  100.7 1.9 %copy.23 = f32[1,64,2048]{2,1,0:T(8,128)} copy(f32[1,64,2048]{2,1,0:T(8,128)} %bitcast.19) | data formatting | bytes 1048576
  102.6 1.9 %copy.24 = f32[1,64,2048]{2,1,0:T(8,128)} copy(f32[1,64,2048]{2,1,0:T(8,128)} %bitcast.18) | data formatting | bytes 1048576
  (5 shorter events, 0.2 us)
Async XLA Ops:
  0.6 18.6 %collective-permute-start = (f32[2048,64]{0,1:T(8,128)}, f32[2048,64]{0,1:T(8,128)}, u32[]{:S(2)}, u32[]{:S(2)}) collective-permute-start(f32[2048,64]{0,1:T(8,128)} %bitcast.15), channel_id=1, source_target_pairs={{0,31},{1,30},{2,29},{3,28},{4,27},{5,26},{6,25},{7,24},{8,23},{9,... | collective-permute-start | bytes 1572872 | tf_op jit(solution)/shard_map/ppermute | solution.py:559
  24.4 0.8 copy-start
where the time goes:
time: 105 us; the launch traced here: 104 us
  Pallas kernels  73.5 us (70%)
  local copies, waits for them, and re-layouts  14.2 us (14%)
  waiting for transfers between devices  9.12 us (9%)
  starting transfers between devices  6.39 us (6%)
    pallas_call x1, Pallas kernels, shards(): pl.pallas_call(kernel, out_shape=(block, block), in_specs=[vmem] * 8, out...  73.5 us
    ppermute x1, waiting for transfers between devices, arrange_weights(): other = lax.ppermute(w, 'rows', [(i, R - 1 - i) for i in range(R)])  9.12 us
    unnamed x10, local copies, waits for them, and re-layouts  7.1 us
    ppermute x1, starting transfers between devices, arrange_weights(): other = lax.ppermute(w, 'rows', [(i, R - 1 - i) for i in range(R)])  6.39 us
  transfers between devices with their start and end apart: 1, of which 1 were waited for; matrix products, arithmetic and copies ran while one was open for 3% of the time, Pallas kernels for 0%

commit v1 on v0

--- a/solution.py
+++ b/solution.py
@@ -140,6 +140,24 @@
     angle = np.concatenate([angle, angle], axis=1)
     col_twist = np.stack([np.cos(angle), np.sin(angle)])
 
+    flip = np.zeros((2, 2, 128, 128))
+    for kk in range(2):
+        for u in range(64):
+            flip[0, :, 64 * kk + 63 - u, 64 * kk + u] = 1.0
+            flip[1, :, 64 * kk + (64 - u) % 64, 64 * kk + u] = 1.0
+    pick = np.zeros((2, 40, 2, 64))
+    for kk in range(2):
+        for q in range(3):
+            for half in range(2):
+                s = 4 * q + 2 * half + kk
+                k = s + 1 if s < 8 else 0
+                for jj in range(4):
+                    if s < 9:
+                        pick[kk, 8 * q + 4 * half + jj, :, 16 * jj + k] = 2.0**-22
+                    if s < 7:
+                        pick[kk, 24 + 8 * q + 4 * half + jj, :, 16 * (3 - jj) + 16 - k] = 2.0**-22
+    perm = np.concatenate([flip.reshape(512, 128), pick.reshape(80, 128)]).astype(BF16)
+
     def halves(table):
         high = table.astype(BF16)
         return np.stack([high, (table - high.astype(np.float64)).astype(BF16)])
@@ -150,6 +168,7 @@
         halves(cols.T),
         np.asarray(row_twist, np.float32),
         np.asarray(col_twist, np.float32),
+        perm,
     )
 
 
@@ -167,9 +186,10 @@
 
 
 def kernel(
-    est, dirty, weights, row_table, col_table, col_back, row_twist, col_twist,
-    new_ref, res_ref,
-    abuf, send, recv, spec, send2, recv2, hz, hr, det, energy, ob, mx_own, mx_z, mx_r,
+    est, dirty, psf, row_table, col_table, col_back, row_twist, col_twist, perm,
+    shrink_ref, blur_ref,
+    abuf, send, recv, spec, send2, recv2, hz, hh, hp, hpr, hr, det, energy, ob, mx_own, mx_z, mx_r,
+    weights, mirror, flipped, mirror_in, w_send, w_recv, p_send, p_recv,
     s_send, s_recv, s_send2, s_recv2, z_send, z_recv, h_send, h_recv, o_send, o_recv,
     mz_send, mz_recv, mr_send, mr_recv, own_sem,
 ):
@@ -225,7 +245,45 @@
 
     pl.semaphore_wait(barrier, R - 1 + Z - 1)
 
-    def exchange(source, target, send_sem, recv_sem):
+    partner = pltpu.make_async_remote_copy(
+        src_ref=flipped,
+        dst_ref=mirror_in,
+        send_sem=w_send,
+        recv_sem=w_recv,
+        device_id={"rows": R - 1 - p},
+        device_id_type=MESH,
+    )
+    left_half = lax.broadcasted_iota(jnp.int32, (40, 128), 1) < 64
+
+    def arrange_weights():
+        for i in range(8):
+            rows = [psf[pl.ds(4 * i + n, 64, stride=32), :] for n in range(4)]
+            high, low = split(jnp.concatenate(rows, axis=0))
+            both = jnp.concatenate([high, low], axis=1)
+            out = lax.dot_general(
+                perm[512:592], both, (((1,), (1,)), ((), ())), preferred_element_type=F32
+            )
+            for n in range(2):
+                a = out[0:40, 128 * n : 128 * n + 128]
+                b = out[40:80, 128 * n : 128 * n + 128]
+                first = jnp.where(left_half, a, roll(b, 64, 1))
+                second = jnp.where(left_half, roll(a, 64, 1), b)
+                for u1, value in ((4 * i + 2 * n, first), (4 * i + 2 * n + 1, second)):
+                    for q in range(3):
+                        weights[q, u1] = value[8 * q : 8 * q + 8]
+                    for q in range(2):
+                        mirror[q, u1] = value[24 + 8 * q : 32 + 8 * q]
+        for q in range(2):
+            high, low = split(mirror[q].reshape(256, 128))
+            both = jnp.concatenate([high, low], axis=1)
+            out = jnp.dot(both, perm[0:256], preferred_element_type=F32)
+            zero = jnp.dot(both[0:16], perm[256:512], preferred_element_type=F32)
+            flipped[q, 0] = zero[0:8]
+            for u1 in range(1, 32):
+                flipped[q, 32 - u1] = out[8 * u1 : 8 * u1 + 8]
+        partner.start()
+
+    def exchange(source, target, send_sem, recv_sem, between):
         def copy(to, slot, sem):
             return pltpu.make_async_remote_copy(
                 src_ref=source.at[to],
@@ -243,6 +301,7 @@
         lax.fori_loop(1, R, begin, 0)
         own = pltpu.make_async_copy(source.at[p], target.at[p, 0:TILES], own_sem)
         own.start()
+        between()
 
         def end(i, carry):
             other = lax.rem(p + R - i, R)
@@ -259,7 +318,11 @@
 
         lax.fori_loop(1, R, sent, 0)
 
-    exchange(send, recv, s_send, s_recv)
+    exchange(send, recv, s_send, s_recv, arrange_weights)
+    partner.wait_recv()
+    partner.wait_send()
+    for q in range(2):
+        weights[q] = weights[q] + mirror_in[q]
 
     recv[:, TILES] = jnp.zeros((R, 8, 128), F32)
     upper = lax.broadcasted_iota(jnp.int32, (8, 128), 0) < 4
@@ -321,16 +384,17 @@
     lax.fori_loop(1, R, end2, 0)
     own2.wait()
 
+    def sent2(i, carry):
+        copy2(lax.rem(p + i, R), p, p).wait_send()
+        return carry
+
+    lax.fori_loop(1, R, sent2, 0)
+
     for t in range(TILES):
         block = recv2[:, t].reshape(256, 128)
         abuf[128 * t : 128 * t + 128, :] = dot3(split(block), table, ((0,), (0,)))
 
-    for c in range(Z):
-        if c == 0:
-            hz[c, :, 0:128] = jnp.zeros((64, 128), F32)
-        if c == Z - 1:
-            hz[c, :, 640:768] = jnp.zeros((64, 128), F32)
-
+    left_lanes = lax.broadcasted_iota(jnp.int32, (8, 128), 1) < 64
     def rows_inverse(g, carry):
         re, im = [None] * 9, [None] * 8
         for k in range(1, 9):
@@ -345,6 +409,7 @@
         cosine = cosine_16(re[0], re[8], re)
         sine = sine_16(im)
         at = pl.ds(pl.multiple_of(8 * g, 8), 8)
+        edges = {}
         for a in range(16):
             if a == 0 or a == 8:
                 blurred = cosine[a]
@@ -353,23 +418,40 @@
             else:
                 blurred = cosine[16 - a] + sine[16 - a]
             lanes = slice(128 * a, 128 * a + 128)
-            residual = dirty[at, lanes] - blurred
-            res_ref[at, lanes] = residual
-            halfway = est[at, lanes] + step_size * residual
-            own = a // 4
-            hz[own, at, 128 * (a % 4) + 128 : 128 * (a % 4) + 256] = halfway
-            if a % 4 == 0 and own > 0:
-                hz[own - 1, at, 640:768] = halfway
-            if a % 4 == 3 and own < Z - 1:
-                hz[own + 1, at, 0:128] = halfway
+            blur_ref[at, lanes] = blurred
+            halfway = est[at, lanes] + step_size * (dirty[at, lanes] - blurred)
+            hz[a // 4, at, 128 * (a % 4) : 128 * (a % 4) + 128] = halfway
+            if a % 4 in (0, 3):
+                edges[a] = halfway
+        for c in range(Z):
+            right = edges[4 * c + 4] if c < Z - 1 else jnp.zeros((8, 128), F32)
+            left = edges[4 * c - 1] if c > 0 else jnp.zeros((8, 128), F32)
+            hh[c, at, :] = roll(jnp.where(left_lanes, right, left), 16, 1)
         return carry
 
     lax.fori_loop(0, 8, rows_inverse, 0)
+
+    lane_group = lax.broadcasted_iota(jnp.int32, (16, 128), 1) // 32
+    for c in range(Z):
+        packed = hh[c, 0:16, :]
+        for g in range(1, 4):
+            packed = jnp.where(lane_group == g, roll(hh[c, 16 * g : 16 * g + 16, :], 32 * g, 1), packed)
+        hp[c] = packed
+
+    def copy_p(to, slot, sem):
+        return pltpu.make_async_remote_copy(
+            src_ref=hp.at[to],
+            dst_ref=hpr.at[slot],
+            send_sem=p_send.at[to],
+            recv_sem=p_recv.at[sem],
+            device_id={"chan": to},
+            device_id_type=MESH,
+        )
 
     def copy_z(to, slot, sem):
         return pltpu.make_async_remote_copy(
             src_ref=hz.at[to],
-            dst_ref=hr.at[slot, 16:80, :],
+            dst_ref=hr.at[slot, 16:80, 0:512],
             send_sem=z_send.at[to],
             recv_sem=z_recv.at[sem],
             device_id={"chan": to},
@@ -377,22 +459,31 @@
         )
 
     for i in range(1, Z):
+        copy_p(lax.rem(z + i, Z), z, z).start()
         copy_z(lax.rem(z + i, Z), z, z).start()
-    own3 = pltpu.make_async_copy(hz.at[z], hr.at[z, 16:80, :], own_sem)
+    own3 = pltpu.make_async_copy(hz.at[z], hr.at[z, 16:80, 0:512], own_sem)
     own3.start()
+    hpr[z] = hp[z]
 
     @pl.when(p == 0)
     def _():
-        hr[:, 0:16, :] = jnp.zeros((Z, 16, 768), F32)
+        hr[:, 0:16, :] = jnp.zeros((Z, 16, 640), F32)
 
     @pl.when(p == R - 1)
     def _():
-        hr[:, 80:96, :] = jnp.zeros((Z, 16, 768), F32)
+        hr[:, 80:96, :] = jnp.zeros((Z, 16, 640), F32)
 
     for i in range(1, Z):
         other = lax.rem(z + Z - i, Z)
+        copy_p(other, other, other).wait_recv()
         copy_z(other, other, other).wait_recv()
     own3.wait()
+    for i in range(1, Z):
+        copy_p(lax.rem(z + i, Z), z, z).wait_send()
+        copy_z(lax.rem(z + i, Z), z, z).wait_send()
+    for c in range(Z):
+        for g in range(4):
+            hr[c, 16 + 16 * g : 32 + 16 * g, 512:640] = roll(hpr[c], -32 * g - 16, 1)
 
     above = pltpu.make_async_remote_copy(
         src_ref=hr.at[:, 16:32, :],
@@ -426,11 +517,19 @@
     @pl.when(p > 0)
     def _():
         below.wait_recv()
+        above.wait_send()
+
+    @pl.when(p < R - 1)
+    def _():
+        below.wait_send()
+
 
     row_ids = lax.broadcasted_iota(jnp.int32, (96, 1), 0) + 64 * p - 16
-    col_ids = lax.broadcasted_iota(jnp.int32, (1, 768), 1) + 512 * z - 128
     row_mask = jnp.logical_and(row_ids >= 0, row_ids < 64 * R).astype(F32)
-    col_mask = jnp.logical_and(col_ids >= 0, col_ids < 512 * Z).astype(F32)
+    col_ids = lax.broadcasted_iota(jnp.int32, (1, 640), 1)
+    right_zero = jnp.logical_and(z == Z - 1, jnp.logical_and(col_ids >= 512, col_ids < 576))
+    left_zero = jnp.logical_and(z == 0, col_ids >= 576)
+    col_mask = 1.0 - jnp.logical_or(right_zero, left_zero).astype(F32)
 
     def starlet(ch, carry):
         current = hr[ch]
@@ -438,7 +537,7 @@
             later = smooth(current, 1 << level)
             if level < 2:
                 later = later * row_mask * col_mask
-            detail = (current - later)[16:80, 128:640]
+            detail = (current - later)[16:80, 0:512]
             det[level, ch] = detail
             squared = detail * detail
             energy[level] = jnp.where(ch == 0, squared, energy[level] + squared)
@@ -507,83 +606,51 @@
     def copy_o(to, slot, sem):
         return pltpu.make_async_remote_copy(
             src_ref=ob.at[to],
-            dst_ref=new_ref.at[:, pl.ds(pl.multiple_of(512 * slot, 512), 512)],
+            dst_ref=shrink_ref.at[:, pl.ds(pl.multiple_of(512 * slot, 512), 512)],
             send_sem=o_send.at[to],
             recv_sem=o_recv.at[sem],
             device_id={"chan": to},
             device_id_type=MESH,
         )
 
+    def shrunk(ch):
+        out = energy[0] * det[0, ch]
+        out = out + energy[1] * det[1, ch]
+        return out + energy[2] * det[2, ch]
+
     def final(i, carry):
         ch = lax.rem(z + i, Z)
-        out = hr[ch, 16:80, 128:640]
-        for level in range(3):
-            out = out - energy[level] * det[level, ch]
-        ob[ch] = out
+        ob[ch] = shrunk(ch)
         copy_o(ch, z, z).start()
         return carry
 
     lax.fori_loop(1, Z, final, 0)
-    out = hr[z, 16:80, 128:640]
-    for level in range(3):
-        out = out - energy[level] * det[level, z]
-    new_ref[:, pl.ds(pl.multiple_of(512 * z, 512), 512)] = out
-
-    def sent2(i, carry):
-        to = lax.rem(p + i, R)
-        copy2(to, p, p).wait_send()
-        copy_mr(to, p).wait_send()
-        return carry
-
-    lax.fori_loop(1, R, sent2, 0)
-
-    @pl.when(p > 0)
-    def _():
-        above.wait_send()
-
-    @pl.when(p < R - 1)
-    def _():
-        below.wait_send()
+    shrink_ref[:, pl.ds(pl.multiple_of(512 * z, 512), 512)] = shrunk(z)
+
+    def sent3(i, carry):
+        copy_mr(lax.rem(p + i, R), p).wait_send()
+        return carry
+
+    lax.fori_loop(1, R, sent3, 0)
 
     for i in range(1, Z):
         other = lax.rem(z + Z - i, Z)
         copy_o(other, other, other).wait_recv()
     for i in range(1, Z):
         to = lax.rem(z + i, Z)
-        copy_z(to, z, z).wait_send()
         copy_mz(to, z).wait_send()
         copy_o(to, z, z).wait_send()
 
 
-def arrange_weights(w):
-    other = lax.ppermute(w, "rows", [(i, R - 1 - i) for i in range(R)])
-    mirror = jnp.roll(jnp.flip(other, axis=0), 1, axis=0)
-    mirror = jnp.roll(jnp.flip(mirror, axis=1), 1, axis=1)
-    w4 = w.reshape(64, 32, 4, 16)
-    m4 = mirror.reshape(64, 32, 4, 16)
-    both = jnp.concatenate(
-        [
-            w4[..., 1:8] + m4[..., 1:8],
-            w4[..., 8:9],
-            w4[..., 0:1],
-            jnp.zeros((64, 32, 4, 3), F32),
-        ],
-        axis=3,
-    ) * (1.0 / (2048.0 * 2048.0))
-    both = both.reshape(64, 32, 4, 3, 2, 2)
-    return both.transpose(3, 1, 4, 2, 5, 0).reshape(3, 32, 8, 128)
-
-
 def shards(estimate, dirty_image, psf_weights):
-    weights = arrange_weights(psf_weights[0])
     constants = tables()
     vmem = pl.BlockSpec(memory_space=pltpu.VMEM)
     block = jax.ShapeDtypeStruct((64, 2048), F32)
     dma = pltpu.SemaphoreType.DMA
-    new, res = pl.pallas_call(
+    shrink, blurred = pl.pallas_call(
         kernel,
         out_shape=(block, block),
-        in_specs=[vmem] * 8,
+        in_specs=[vmem] * 9,
         out_specs=(vmem, vmem),
         scratch_shapes=[
             pltpu.VMEM((640, 256), F32),
@@ -592,21 +659,31 @@
             pltpu.VMEM((256, 256), F32),
             pltpu.VMEM((R, TILES + 1, 8, 128), F32),
             pltpu.VMEM((R, TILES, 8, 128), F32),
-            pltpu.VMEM((Z, 64, 768), F32),
-            pltpu.VMEM((Z, 96, 768), F32),
+            pltpu.VMEM((Z, 64, 512), F32),
+            pltpu.VMEM((Z, 64, 128), F32),
+            pltpu.VMEM((Z, 16, 128), F32),
+            pltpu.VMEM((Z, 16, 128), F32),
+            pltpu.VMEM((Z, 96, 640), F32),
             pltpu.VMEM((3, Z, 64, 512), F32),
             pltpu.VMEM((3, 64, 512), F32),
             pltpu.VMEM((Z, 64, 512), F32),
             pltpu.VMEM((2, 1, 128), F32),
             pltpu.VMEM((Z, 1, 128), F32),
             pltpu.VMEM((R, 1, 128), F32),
+            pltpu.VMEM((3, 32, 8, 128), F32),
+            pltpu.VMEM((2, 32, 8, 128), F32),
+            pltpu.VMEM((2, 32, 8, 128), F32),
+            pltpu.VMEM((2, 32, 8, 128), F32),
+            dma, dma, dma((Z,)), dma((Z,)),
             dma((R,)), dma((R,)), dma((R,)), dma((R,)),
             dma((Z,)), dma((Z,)), dma((2,)), dma((2,)), dma((Z,)), dma((Z,)),
             dma((Z,)), dma((Z,)), dma((R,)), dma((R,)), dma,
         ],
         compiler_params=pltpu.CompilerParams(collective_id=0, has_side_effects=True),
-    )(estimate[0], dirty_image[0], weights, *constants)
-    return (new[None], res[None])
+    )(estimate[0], dirty_image[0], psf_weights[0], *constants)
+    residual = dirty_image[0] - blurred
+    new = estimate[0] + step_size * residual - shrink
+    return (new[None], residual[None])
 
 
 def solution(mesh):

time: 105 us -> 83.9 us (0.80)
  local copies, waits for them, and re-layouts: 14.2 us -> 2.36 us
  waiting for transfers between devices: 9.12 us -> 0 us
  starting transfers between devices: 6.39 us -> 0 us
  Pallas kernels: 73.5 us -> 78.4 us
  other arithmetic: 0.48 us -> 2.28 us
    ppermute x1 -> x0, waiting for transfers between devices: 9.12 us -> none  [arrange_weights(): other = lax.ppermute(w, 'rows', [(i, R - 1 - i) for i in range(R)])]
    ppermute x1 -> x0, starting transfers between devices: 6.39 us -> none  [arrange_weights(): other = lax.ppermute(w, 'rows', [(i, R - 1 - i) for i in range(R)])]
    pallas_call x1, Pallas kernels: 73.5 us -> 78.4 us  [shards(): pl.pallas_call(kernel, out_shape=(block, block), in_specs=[vmem] * 9, out...]
    unnamed x10 -> x5, local copies, waits for them, and re-layouts: 7.1 us -> 2.36 us
    slice x6 -> x0, local copies, waits for them, and re-layouts: 2.73 us -> none  [the longest x2 2 us: arrange_weights(): mirror = jnp.roll(jnp.flip(other, axis=0), 1, axis=0)]
    broadcast_in_dim x0 -> x1, other arithmetic: none -> 2.28 us  [shards(): return (new[None], residual[None])]
    reshape x2 -> x0, local copies, waits for them, and re-layouts: 1.88 us -> none  [the longest x1 1.2 us: arrange_weights(): return both.transpose(3, 1, 4, 2, 5, 0).reshape(3, 32, 8, 128)]
    another operation x1 -> x0, local copies, waits for them, and re-layouts: 1.81 us -> none  [arrange_weights(): w4 = w.reshape(64, 32, 4, 16)]
  transfers between devices with their start and end apart: 1 -> 0, of which waited for: 1 -> 0; matrix products, arithmetic and copies ran while one was open for 3% -> 0% of each run, Pallas kernels for 0% -> 0%
where the time goes in v1:
time: 83.9 us; the launch traced here: 83.7 us
  Pallas kernels  78.4 us (93%)
  local copies, waits for them, and re-layouts  2.36 us (3%)
  other arithmetic  2.28 us (3%)
    pallas_call x1, Pallas kernels, shards(): pl.pallas_call(kernel, out_shape=(block, block), in_specs=[vmem] * 9, out...  78.4 us
    unnamed x5, local copies, waits for them, and re-layouts  2.36 us
    broadcast_in_dim x1, other arithmetic, shards(): return (new[None], residual[None])  2.28 us

profile of v1, /device:TPU:1, one launch (start us, length us, event | category | flops | bytes accessed | tf_op | source)
XLA Modules:
  0.0 83.7 jit_solution(16178638226375546459)
XLA Ops:
  0.6 2.3 %copy.11 = f32[1,2048,64]{2,1,0:T(8,128)} copy(f32[1,2048,64]{1,2,0:T(8,128)} %param.11) | data formatting | bytes 1048576 | tf_op args[2]
  3.0 0.0 copy-start
  3.0 0.0 copy-start.1
  3.0 78.4 %shard_map.104 = (f32[64,2048]{1,0:T(8,128)}, f32[64,2048]{1,0:T(8,128)}) custom-call(f32[64,2048]{1,0:T(8,128)} %bitcast.11, f32[64,2048]{1,0:T(8,128)} %bitcast.12, f32[2048,64]{1,0:T(8,128)} %bitcast.10, bf16[2,256,256]{2,1,0:T(8,128)(2,1)} %constant.14.clone.row_table, bf16[2,256,256]{2,1,0:T(8,128)(2,1)} %constant.15.clone.col_table, ...), custom_call_target="tpu_custom_call" | custom-call | tf_op jit(solution)/shard_map/pallas_call | solution.py:650
  81.4 0.0 copy-done
  81.4 0.0 copy-done.1
  81.4 2.3 %subtract_bitcast_fusion.1 = (f32[1,64,2048]{2,1,0:T(8,128)}, f32[1,64,2048]{2,1,0:T(8,128)}) fusion(f32[64,2048]{1,0:T(8,128)} %get-tuple-element.4, f32[1,64,2048]{2,1,0:T(8,128)S(1)} %copy-done.1, f32[64,2048]{1,0:T(8,128)} %get-tuple-element.5, f32[1,64,2048]{2,1,0:T(8,128)S(1)} %copy-done), kind=kLoop, calls=%fused_computation.1 | loop fusion | flops 524288 | bytes 3145728 | tf_op jit(solution)/shard_map/broadcast_in_dim | solution.py:686
Async XLA Ops:
  3.0 78.4 %copy-start = (f32[1,64,2048]{2,1,0:T(8,128)S(1)}, f32[1,64,2048]{2,1,0:T(8,128)}, u32[]{:S(2)}) copy-start(f32[1,64,2048]{2,1,0:T(8,128)} %param.9) | copy-start | bytes 1572868
  3.0 78.4 %copy-start.1 = (f32[1,64,2048]{2,1,0:T(8,128)S(1)}, f32[1,64,2048]{2,1,0:T(8,128)}, u32[]{:S(2)}) copy-start(f32[1,64,2048]{2,1,0:T(8,128)} %param.10) | copy-start | bytes 1572868

commit v2 on v1

v2 whole, which is shorter than its diff:
```python
import functools
import math

import jax
import jax.numpy as jnp
import numpy as np
from jax import lax
from jax.experimental import pallas as pl
from jax.experimental.pallas import tpu as pltpu
from jax.sharding import PartitionSpec as P

fractions = (0.03, 0.02, 0.015)
step_size = 0.9
MESH = pl.DeviceIdType.MESH
F32 = jnp.float32
BF16 = jnp.bfloat16
R = 32
Z = 4
VMEM_LIMIT = 60 * 1024 * 1024
TILES = 5


def linear(pairs):
    total = None
    for coef, value in pairs:
        if abs(coef) < 1e-12:
            continue
        if abs(coef - 1.0) < 1e-12:
            total = value if total is None else total + value
        elif abs(coef + 1.0) < 1e-12:
            total = -value if total is None else total - value
        else:
            term = coef * value
            total = term if total is None else total + term
    return total


def cosine_16(first, middle, e):
    out = [None] * 9
    for k in range(5):
        even = linear(
            [(1.0, first), (1.0 if k % 2 == 0 else -1.0, middle)]
            + [(math.cos(2 * math.pi * k * a / 16), e[a]) for a in (2, 4, 6)]
        )
        odd = linear([(math.cos(2 * math.pi * k * a / 16), e[a]) for a in (1, 3, 5, 7)])
        if odd is None:
            out[k] = even
            out[8 - k] = even
        else:
            out[k] = even + odd
            out[8 - k] = even - odd
    return out


def sine_16(o):
    out = [None] * 8
    for k in range(1, 5):
        even = linear([(math.sin(2 * math.pi * k * a / 16), o[a]) for a in (2, 4, 6)])
        odd = linear([(math.sin(2 * math.pi * k * a / 16), o[a]) for a in (1, 3, 5, 7)])
        if even is None:
            out[k] = odd
        else:
            out[k] = odd + even
            out[8 - k] = odd - even
    return out


def fft(values, sign):
    count = len(values)
    if count == 1:
        return values
    if count == 2:
        (ar, ai), (br, bi) = values
        return [(ar + br, ai + bi), (ar - br, ai - bi)]
    if count == 4:
        (ar, ai), (br, bi), (cr, ci), (dr, di) = values
        sr, si, tr, ti = ar + cr, ai + ci, ar - cr, ai - ci
        ur, ui, vr, vi = br + dr, bi + di, br - dr, bi - di
        if sign > 0:
            return [(sr + ur, si + ui), (tr - vi, ti + vr), (sr - ur, si - ui), (tr + vi, ti - vr)]
        return [(sr + ur, si + ui), (tr + vi, ti - vr), (sr - ur, si - ui), (tr - vi, ti + vr)]
    quarter = count // 4
    parts = [fft(values[n::4], sign) for n in range(4)]
    out = [None] * count
    for k in range(quarter):
        four = []
        for n in range(4):
            re, im = parts[n][k]
            angle = sign * 2 * math.pi * n * k / count
            c, s = math.cos(angle), math.sin(angle)
            if n * k == 0:
                four.append((re, im))
            elif abs(abs(c) - abs(s)) < 1e-9:
                h = abs(c)
                cs, ss = math.copysign(1, c), math.copysign(1, s)
                r = (re if cs > 0 else -re) - (im if ss > 0 else -im)
                i = (im if cs > 0 else -im) + (re if ss > 0 else -re)
                four.append((h * r, h * i))
            else:
                four.append((re * c - im * s, re * s + im * c))
        for m, value in enumerate(fft(four, sign)):
            out[k + m * quarter] = value
    return out


def split(value):
    high = value.astype(BF16)
    return high, (value - high.astype(F32)).astype(BF16)


def dot3(a, b, dims):
    (ah, al), (bh, bl) = a, b
    dot = functools.partial(
        lax.dot_general, dimension_numbers=(dims, ((), ())), preferred_element_type=F32
    )
    return dot(ah, bh) + (dot(al, bh) + dot(ah, bl))


def tables():
    m = np.arange(128)
    rows = np.zeros((256, 256))
    for d in range(32):
        for jj in range(4):
            angle = 2 * np.pi * ((4 * d + jj) * m % 128) / 128
            rows[8 * d + jj] = np.concatenate([np.cos(angle), np.sin(angle)])
            rows[8 * d + 4 + jj] = np.concatenate([-np.sin(angle), np.cos(angle)])
    n = np.arange(64)
    angle = 2 * np.pi * (n[:, None] * n[None, :] % 64) / 64
    cols = np.zeros((2, 2, 64, 2, 2, 64))
    for kk in range(2):
        cols[0, kk, :, 0, kk] = np.cos(angle)
        cols[1, kk, :, 0, kk] = np.sin(angle)
        cols[0, kk, :, 1, kk] = -np.sin(angle)
        cols[1, kk, :, 1, kk] = np.cos(angle)
    cols = cols.reshape(256, 256)
    early = np.concatenate([np.arange(16), np.arange(48, 64)])
    chunk = np.concatenate([early, np.arange(16, 48)]).reshape(2, 32)
    back = cols.T.reshape(256, 2, 2, 64)[:, :, :, chunk]
    back = back.transpose(0, 1, 3, 2, 4).reshape(256, 256)
    k = np.arange(1, 9)
    angle = -2 * np.pi * k[:, None] * m[None, :] / 2048
    row_twist = np.concatenate([np.cos(angle), np.sin(angle)])
    u1 = np.arange(32)
    angle = -2 * np.pi * u1[:, None] * n[None, :] / 2048
    angle = np.concatenate([angle, angle], axis=1)
    lanes = np.broadcast_to(chunk[:, None, :], (2, 2, 32)).reshape(128)
    turned = -2 * np.pi * u1[:, None] * lanes[None, :] / 2048
    col_twist = np.stack([np.cos(angle), np.sin(angle), np.cos(turned), np.sin(turned)])

    flip = np.zeros((2, 2, 128, 128))
    for kk in range(2):
        for u in range(64):
            flip[0, :, 64 * kk + 63 - u, 64 * kk + u] = 1.0
            flip[1, :, 64 * kk + (64 - u) % 64, 64 * kk + u] = 1.0
    pick = np.zeros((2, 40, 2, 64))
    for kk in range(2):
        for q in range(3):
            for half in range(2):
                s = 4 * q + 2 * half + kk
                k = s + 1 if s < 8 else 0
                for jj in range(4):
                    if s < 9:
                        pick[kk, 8 * q + 4 * half + jj, :, 16 * jj + k] = 2.0**-22
                    if s < 7:
                        pick[kk, 24 + 8 * q + 4 * half + jj, :, 16 * (3 - jj) + 16 - k] = 2.0**-22
    perm = np.concatenate([flip.reshape(512, 128), pick.reshape(80, 128)]).astype(BF16)

    def halves(table):
        high = table.astype(BF16)
        return np.stack([high, (table - high.astype(np.float64)).astype(BF16)])

    return (
        halves(rows),
        halves(cols),
        halves(back),
        np.asarray(row_twist, np.float32),
        np.asarray(col_twist, np.float32),
        perm,
    )


def roll(value, shift, axis):
    return pltpu.roll(value, shift % value.shape[axis], axis)


def smooth(value, spacing):
    for axis in (1, 0):
        value = value + roll(value, spacing, axis)
        value = value + roll(value, -spacing, axis)
        value = value + roll(value, spacing, axis)
        value = value + roll(value, -spacing, axis)
    return value * (1.0 / 256.0)


def drain(ref, sem):
    pltpu.make_async_copy(ref, ref, sem).wait()


def kernel(
    est_in, dirty_in, psf_in, row_table_in, col_table_in, col_back_in, row_twist_in, col_twist_in,
    perm_in,
    shrink_ref, blur_ref,
    est, dirty, psf_wide, row_table, col_table, col_back, row_twist, col_twist, perm,
    psf, abuf, send, recv, spec, send_a, send_b, recv_a, recv_b,
    hz, hh, hp, hpr, hr, det, energy, ob, mx_own, mx_z, mx_r,
    weights, mirror, flipped, mirror_in, in_sems, sems,
):
    z = lax.axis_index("chan")
    p = lax.axis_index("rows")

    barrier = pltpu.get_barrier_semaphore()

    def greet_row(i, carry):
        pl.semaphore_signal(
            barrier, inc=1, device_id={"rows": lax.rem(p + i, R)}, device_id_type=MESH
        )
        return carry

    def greet_chan(i, carry):
        pl.semaphore_signal(
            barrier, inc=1, device_id={"chan": lax.rem(z + i, Z)}, device_id_type=MESH
        )
        return carry

    lax.fori_loop(1, R, greet_row, 0)
    lax.fori_loop(1, Z, greet_chan, 0)

    pairs = (
        (est_in, est), (row_twist_in, row_twist), (row_table_in, row_table), (psf_in, psf_wide),
        (perm_in, perm), (col_twist_in, col_twist), (col_table_in, col_table),
        (col_back_in, col_back), (dirty_in, dirty),
    )
    loads = [pltpu.make_async_copy(a, b, in_sems.at[i]) for i, (a, b) in enumerate(pairs)]
    for load in loads:
        load.start()

    def remote(source, target, send_sem, recv_sem, **device):
        return pltpu.make_async_remote_copy(
            src_ref=source,
            dst_ref=target,
            send_sem=sems.at[send_sem],
            recv_sem=sems.at[recv_sem],
            device_id=device,
            device_id_type=MESH,
        )

    abuf[576:640, :] = jnp.zeros((64, 256), F32)
    for load in loads[:3]:
        load.wait()

    def rows_forward(g, carry):
        at = pl.ds(pl.multiple_of(8 * g, 8), 8)
        x = [est[at, 128 * a : 128 * a + 128] for a in range(16)]
        e = [None] + [x[a] + x[16 - a] for a in range(1, 8)]
        o = [None] + [x[a] - x[16 - a] for a in range(1, 8)]
        re = cosine_16(x[0], x[8], e)
        im = sine_16(o)
        for k in range(1, 9):
            c = row_twist[k - 1 : k, :]
            s = row_twist[k + 7 : k + 8, :]
            to = pl.ds(pl.multiple_of(64 * (k - 1) + 8 * g, 8), 8)
            if k < 8:
                abuf[to, 0:128] = re[k] * c + im[k] * s
                abuf[to, 128:256] = re[k] * s - im[k] * c
            else:
                abuf[to, 0:128] = re[k] * c
                abuf[to, 128:256] = re[k] * s
        to = pl.ds(pl.multiple_of(512 + 8 * g, 8), 8)
        abuf[to, 0:128] = re[0]
        abuf[to, 128:256] = jnp.zeros((8, 128), F32)
        return carry

    lax.fori_loop(0, 8, rows_forward, 0)
    table = (row_table[0], row_table[1])
    for t in range(TILES):
        out = dot3(table, split(abuf[128 * t : 128 * t + 128, :]), ((1,), (1,)))
        send[:, t] = out.reshape(R, 8, 128)

    left_half = lax.broadcasted_iota(jnp.int32, (40, 128), 1) < 64
    for load in loads[3:5]:
        load.wait()
    for b in range(16):
        psf[128 * b : 128 * b + 128, :] = jnp.transpose(psf_wide[:, 128 * b : 128 * b + 128])
    for i in range(8):
        rows = [psf[pl.ds(4 * i + n, 64, stride=32), :] for n in range(4)]
        high, low = split(jnp.concatenate(rows, axis=0))
        both = jnp.concatenate([high, low], axis=1)
        out = lax.dot_general(
            perm[512:592], both, (((1,), (1,)), ((), ())), preferred_element_type=F32
        )
        for n in range(2):
            a = out[0:40, 128 * n : 128 * n + 128]
            b = out[40:80, 128 * n : 128 * n + 128]
            first = jnp.where(left_half, a, roll(b, 64, 1))
            second = jnp.where(left_half, roll(a, 64, 1), b)
            for u1, value in ((4 * i + 2 * n, first), (4 * i + 2 * n + 1, second)):
                for q in range(3):
                    weights[q, u1] = value[8 * q : 8 * q + 8]
                for q in range(2):
                    mirror[q, u1] = value[24 + 8 * q : 32 + 8 * q]
    for q in range(2):
        high, low = split(mirror[q].reshape(256, 128))
        both = jnp.concatenate([high, low], axis=1)
        out = jnp.dot(both, perm[0:256], preferred_element_type=F32)
        zero = jnp.dot(both[0:16], perm[256:512], preferred_element_type=F32)
        flipped[q, 0] = zero[0:8]
        for u1 in range(1, 32):
            flipped[q, 32 - u1] = out[8 * u1 : 8 * u1 + 8]

    pl.semaphore_wait(barrier, R - 1 + Z - 1)

    partner = remote(flipped, mirror_in, 0, 1, rows=R - 1 - p)
    partner.start()

    def begin(i, carry):
        to = lax.rem(p + i, R)
        remote(send.at[to], recv.at[p, 0:TILES], 2, 3, rows=to).start()
        return carry

    lax.fori_loop(1, R, begin, 0)
    recv[p, 0:TILES] = send[p]
    recv[:, TILES] = jnp.zeros((R, 8, 128), F32)
    for load in loads[5:]:
        load.wait()
    drain(recv.at[0 : R - 1, 0:TILES], sems.at[3])
    drain(send.at[0 : R - 1], sems.at[2])
    partner.wait_recv()
    partner.wait_send()
    for q in range(2):
        weights[q] = weights[q] + mirror_in[q]

    upper = lax.broadcasted_iota(jnp.int32, (8, 128), 0) < 4
    left = lax.broadcasted_iota(jnp.int32, (8, 128), 1) < 64

    def columns(q, carry):
        values = []
        for i in range(R):
            a = recv[i, 2 * q]
            b = recv[i, 2 * q + 1]
            values.append(
                (jnp.where(upper, a, roll(b, 4, 0)), jnp.where(upper, roll(a, 4, 0), b))
            )
        for u, (re, im) in enumerate(fft(values, -1)):
            c = col_twist[0, u : u + 1, :]
            s = col_twist[1, u : u + 1, :]
            spec[8 * u : 8 * u + 8, 0:128] = re * c - im * s
            spec[8 * u : 8 * u + 8, 128:256] = re * s + im * c
        out = dot3(split(spec[...]), (col_table[0], col_table[1]), ((1,), (0,)))
        w = weights[q].reshape(256, 128)
        out = jnp.concatenate([out[:, 0:128] * w, out[:, 128:256] * w], axis=1)
        spec[...] = dot3(split(out), (col_back[0], col_back[1]), ((1,), (0,)))
        values = []
        for u in range(R):
            c = col_twist[2, u : u + 1, :]
            s = col_twist[3, u : u + 1, :]
            re = spec[8 * u : 8 * u + 8, 0:128]
            im = spec[8 * u : 8 * u + 8, 128:256]
            values.append((re * c + im * s, im * c - re * s))
        whole = jnp.logical_or(left, q == 2)
        for i, (re, im) in enumerate(fft(values, 1)):
            a = jnp.where(upper, re, roll(im, 4, 0))
            b = jnp.where(upper, roll(re, 4, 0), im)
            send_a[i, q] = jnp.where(whole, a, roll(b, 64, 1))
            send_b[i, q] = jnp.where(left, roll(a, 64, 1), b)
        return carry

    lax.fori_loop(0, 3, columns, 0)

    def begin_a(i, carry):
        to = lax.rem(p + i, R)
        remote(send_a.at[to], recv_a.at[p], 4, 5, rows=to).start()
        return carry

    def begin_b(i, carry):
        to = lax.rem(p + i, R)
        remote(send_b.at[to, 0:2], recv_b.at[p], 6, 7, rows=to).start()
        return carry

    lax.fori_loop(1, R, begin_a, 0)
    lax.fori_loop(1, R, begin_b, 0)
    recv_a[p] = send_a[p]
    recv_b[p] = send_b[p, 0:2]

    def rows_inverse(base, spread, first, last):
        def group(g, carry):
            re, im = [None] * 9, [None] * 8
            for k in range(1, 9):
                c = row_twist[k - 1 : k, :]
                s = row_twist[k + 7 : k + 8, :]
                to = pl.ds(pl.multiple_of(base + 32 * (k - 1) + 8 * g, 8), 8)
                gr, gi = abuf[to, 0:128], abuf[to, 128:256]
                re[k] = gr * c + gi * s
                if k < 8:
                    im[k] = gi * c - gr * s
            re[0] = abuf[pl.ds(pl.multiple_of(last + 8 * g, 8), 8), 0:128]
            cosine = cosine_16(re[0], re[8], re)
            sine = sine_16(im)
            at = pl.ds(pl.multiple_of(first + 8 * g + spread * (g // 2), 8), 8)
            edges = {}
            for a in range(16):
                if a == 0 or a == 8:
                    blurred = cosine[a]
                elif a < 8:
                    blurred = cosine[a] - sine[a]
                else:
                    blurred = cosine[16 - a] + sine[16 - a]
                lanes = slice(128 * a, 128 * a + 128)
                blur_ref[at, lanes] = blurred
                halfway = est[at, lanes] + step_size * (dirty[at, lanes] - blurred)
                hz[a // 4, at, 128 * (a % 4) : 128 * (a % 4) + 128] = halfway
                if a % 4 in (0, 3):
                    edges[a] = halfway
            none = jnp.zeros((8, 128), F32)
            for c in range(Z):
                after = edges[4 * c + 4] if c < Z - 1 else none
                before = edges[4 * c - 1] if c > 0 else none
                hh[c, at, :] = roll(jnp.where(left, after, before), 16, 1)
            return carry

        lax.fori_loop(0, 4, group, 0)

    lane_16 = lax.broadcasted_iota(jnp.int32, (16, 128), 1)

    def pack(half, groups):
        for c in range(Z):
            a, b = (hh[c, 16 * g : 16 * g + 16, :] for g in groups)
            hp[half, c] = jnp.where(lane_16 < 32, a, roll(b, 32, 1))

    def unpack(half, groups):
        for c in range(Z):
            for e, g in enumerate(groups):
                hr[c, 16 + 16 * g : 32 + 16 * g, 512:640] = roll(hpr[half, c], -32 * e - 16, 1)

    drain(recv_a.at[0 : R - 1], sems.at[5])
    for t in range(3):
        block = recv_a[:, t].reshape(256, 128)
        abuf[128 * t : 128 * t + 128, :] = dot3(split(block), table, ((0,), (0,)))
    rows_inverse(0, 32, 0, 256)
    pack(0, (0, 3))
    for i in range(1, Z):
        to = lax.rem(z + i, Z)
        for r in (0, 48):
            rows = slice(r, r + 16)
            remote(
                hz.at[to, rows], hr.at[z, r + 16 : r + 32, 0:512], 8, 9, chan=to
            ).start()
        remote(hp.at[0, to], hpr.at[0, z], 10, 11, chan=to).start()

    drain(recv_b.at[0 : R - 1], sems.at[7])
    for t in range(2):
        block = recv_b[:, t].reshape(256, 128)
        abuf[384 + 128 * t : 512 + 128 * t, :] = dot3(split(block), table, ((0,), (0,)))
    rows_inverse(384, 0, 16, 320)
    pack(1, (1, 2))
    for i in range(1, Z):
        to = lax.rem(z + i, Z)
        remote(hz.at[to, 16:48], hr.at[z, 32:64, 0:512], 12, 13, chan=to).start()
        remote(hp.at[1, to], hpr.at[1, z], 14, 15, chan=to).start()
    drain(send_a.at[0 : R - 1], sems.at[4])
    drain(send_b.at[0 : R - 1, 0:2], sems.at[6])
    hr[z, 16:80, 0:512] = hz[z]
    hpr[:, z] = hp[:, z]

    @pl.when(p == 0)
    def _():
        hr[:, 0:16, :] = jnp.zeros((Z, 16, 640), F32)

    @pl.when(p == R - 1)
    def _():
        hr[:, 80:96, :] = jnp.zeros((Z, 16, 640), F32)

    drain(hz.at[0 : Z - 1, 0:32], sems.at[9])
    drain(hp.at[0, 0 : Z - 1], sems.at[11])
    unpack(0, (0, 3))
    above = remote(hr.at[:, 16:32, :], hr.at[:, 80:96, :], 16, 17, rows=lax.rem(p + R - 1, R))
    below = remote(hr.at[:, 64:80, :], hr.at[:, 0:16, :], 18, 19, rows=lax.rem(p + 1, R))

    @pl.when(p > 0)
    def _():
        above.start()

    @pl.when(p < R - 1)
    def _():
        below.start()

    drain(hz.at[0 : Z - 1, 0:32], sems.at[13])
    drain(hp.at[0, 0 : Z - 1], sems.at[15])
    unpack(1, (1, 2))
    drain(hz.at[0 : Z - 1, 0:32], sems.at[8])
    drain(hp.at[0, 0 : Z - 1], sems.at[10])
    drain(hz.at[0 : Z - 1, 0:32], sems.at[12])
    drain(hp.at[0, 0 : Z - 1], sems.at[14])

    @pl.when(p < R - 1)
    def _():
        above.wait_recv()

    @pl.when(p > 0)
    def _():
        below.wait_recv()
        above.wait_send()

    @pl.when(p < R - 1)
    def _():
        below.wait_send()


    row_ids = lax.broadcasted_iota(jnp.int32, (96, 1), 0) + 64 * p - 16
    row_mask = jnp.logical_and(row_ids >= 0, row_ids < 64 * R).astype(F32)
    col_ids = lax.broadcasted_iota(jnp.int32, (1, 640), 1)
    right_zero = jnp.logical_and(z == Z - 1, jnp.logical_and(col_ids >= 512, col_ids < 576))
    left_zero = jnp.logical_and(z == 0, col_ids >= 576)
    col_mask = 1.0 - jnp.logical_or(right_zero, left_zero).astype(F32)

    def starlet(ch, carry):
        current = hr[ch]
        for level in range(3):
            later = smooth(current, 1 << level)
            if level < 2:
                later = later * row_mask * col_mask
            detail = (current - later)[16:80, 0:512]
            det[level, ch] = detail
            energy[level] = energy[level] + detail * detail
            current = later
        return carry

    energy[...] = jnp.zeros((3, 64, 512), F32)
    lax.fori_loop(0, Z, starlet, 0)

    lane = lax.broadcasted_iota(jnp.int32, (1, 128), 1)
    peaks = jnp.zeros((1, 128), F32)
    for level in range(3):
        peaks = jnp.where(lane == level, jnp.max(energy[level]), peaks)
    mx_own[0] = peaks
    for i in range(1, Z):
        remote(mx_own.at[0], mx_z.at[z], 20, 21, chan=lax.rem(z + i, Z)).start()
    mx_z[z] = peaks
    drain(mx_z.at[0 : Z - 1], sems.at[21])
    peaks = jnp.max(mx_z[...], axis=0)
    mx_own[1] = peaks

    def begin_max(i, carry):
        remote(mx_own.at[1], mx_r.at[p], 22, 23, rows=lax.rem(p + i, R)).start()
        return carry

    lax.fori_loop(1, R, begin_max, 0)
    mx_r[p] = peaks
    energy[...] = lax.rsqrt(energy[...])
    drain(mx_r.at[0 : R - 1], sems.at[23])
    drain(mx_r.at[0 : R - 1], sems.at[22])
    drain(mx_z.at[0 : Z - 1], sems.at[20])
    peaks = jnp.sqrt(jnp.max(mx_r[...], axis=0))
    for level in range(3):
        threshold = fractions[level] * jnp.max(jnp.where(lane == level, peaks, 0.0))
        energy[level] = jnp.minimum(energy[level] * threshold, 1.0)

    def shrunk(ch):
        out = energy[0] * det[0, ch]
        out = out + energy[1] * det[1, ch]
        return out + energy[2] * det[2, ch]

    block = pl.ds(pl.multiple_of(512 * z, 512), 512)

    def final(i, carry):
        ch = lax.rem(z + i, Z)
        ob[ch] = shrunk(ch)
        remote(ob.at[ch], shrink_ref.at[:, block], 24, 25, chan=ch).start()
        return carry

    lax.fori_loop(1, Z, final, 0)
    shrink_ref[:, block] = shrunk(z)
    drain(ob.at[0 : Z - 1], sems.at[25])
    drain(ob.at[0 : Z - 1], sems.at[24])


def shards(estimate, dirty_image, psf_weights):
    constants = tables()
    arguments = (estimate[0], dirty_image[0], psf_weights[0].T, *constants)
    anywhere = pl.BlockSpec(memory_space=pl.ANY)
    vmem = pl.BlockSpec(memory_space=pltpu.VMEM)
    block = jax.ShapeDtypeStruct((64, 2048), F32)
    dma = pltpu.SemaphoreType.DMA
    shapes = [
        (2048, 64),
        (640, 256),
        (R, TILES, 8, 128),
        (R, TILES + 1, 8, 128),
        (256, 256),
        (R, 3, 8, 128),
        (R, 3, 8, 128),
        (R, 3, 8, 128),
        (R, 2, 8, 128),
        (Z, 64, 512),
        (Z, 64, 128),
        (2, Z, 16, 128),
        (2, Z, 16, 128),
        (Z, 96, 640),
        (3, Z, 64, 512),
        (3, 64, 512),
        (Z, 64, 512),
        (2, 1, 128),
        (Z, 1, 128),
        (R, 1, 128),
        (3, 32, 8, 128),
        (2, 32, 8, 128),
        (2, 32, 8, 128),
        (2, 32, 8, 128),
    ]
    shrink, blurred = pl.pallas_call(
        kernel,
        out_shape=(block, block),
        in_specs=[anywhere] * len(arguments),
        out_specs=(vmem, vmem),
        scratch_shapes=[pltpu.VMEM(a.shape, a.dtype) for a in arguments]
        + [pltpu.VMEM(shape, F32) for shape in shapes]
        + [dma((len(arguments),)), dma((26,))],
        compiler_params=pltpu.CompilerParams(
            collective_id=0, has_side_effects=True, vmem_limit_bytes=VMEM_LIMIT
        ),
    )(*arguments)
    residual = dirty_image[0] - blurred
    new = estimate[0] + step_size * residual - shrink
    return (new[None], residual[None])


def solution(mesh):
    return jax.shard_map(
        shards,
        mesh=mesh,
        in_specs=(P("chan", "rows", None), P("chan", "rows", None), P("chan", None, "rows")),
        out_specs=(P("chan", "rows", None), P("chan", "rows", None)),
        check_vma=False,
    )
```

time: 83.9 us -> 73.6 us (0.88)
  Pallas kernels: 78.4 us -> 70.5 us
  local copies, waits for them, and re-layouts: 2.36 us -> 0.01 us
    pallas_call x1, Pallas kernels: 78.4 us -> 70.5 us  [shards(): pl.pallas_call(kernel, out_shape=(block, block), in_specs=[anywhere] * le...]
    unnamed x5 -> x4, local copies, waits for them, and re-layouts: 2.36 us -> 0.01 us
where the time goes in v2:
time: 73.6 us; the launch traced here: 73.5 us
  Pallas kernels  70.5 us (96%)
  other arithmetic  2.3 us (3%)
    pallas_call x1, Pallas kernels, shards(): pl.pallas_call(kernel, out_shape=(block, block), in_specs=[anywhere] * le...  70.5 us
    broadcast_in_dim x1, other arithmetic, shards(): return (new[None], residual[None])  2.3 us

profile of v2, /device:TPU:1, one launch (start us, length us, event | category | flops | bytes accessed | tf_op | source)
XLA Modules:
  0.0 73.5 jit_solution(14119518610246755910)
XLA Ops:
  0.6 0.0 copy-start
  0.6 0.0 copy-start.1
  0.6 70.5 %shard_map.104 = (f32[64,2048]{1,0:T(8,128)}, f32[64,2048]{1,0:T(8,128)}) custom-call(f32[64,2048]{1,0:T(8,128)} %bitcast.12, f32[64,2048]{1,0:T(8,128)} %bitcast.13, f32[64,2048]{1,0:T(8,128)} %bitcast.14, bf16[2,256,256]{2,1,0:T(8,128)(2,1)} %constant.14.clone.row_table_in, bf16[2,256,256]{2,1,0:T(8,128)(2,1)} %constant.15.clone.col_table_in, ...), custom_call_target="tpu_custom_call" | custom-call | tf_op jit(solution)/shard_map/pallas_call | solution.py:609
  71.2 0.0 copy-done
  71.2 0.0 copy-done.1
  71.2 2.3 %subtract_bitcast_fusion.1 = (f32[1,64,2048]{2,1,0:T(8,128)}, f32[1,64,2048]{2,1,0:T(8,128)}) fusion(f32[64,2048]{1,0:T(8,128)} %get-tuple-element.4, f32[1,64,2048]{2,1,0:T(8,128)S(1)} %copy-done.1, f32[64,2048]{1,0:T(8,128)} %get-tuple-element.5, f32[1,64,2048]{2,1,0:T(8,128)S(1)} %copy-done), kind=kLoop, calls=%fused_computation.1 | loop fusion | flops 524288 | bytes 3145728 | tf_op jit(solution)/shard_map/broadcast_in_dim | solution.py:623
Async XLA Ops:
  0.6 70.5 %copy-start = (f32[1,64,2048]{2,1,0:T(8,128)S(1)}, f32[1,64,2048]{2,1,0:T(8,128)}, u32[]{:S(2)}) copy-start(f32[1,64,2048]{2,1,0:T(8,128)} %param.9) | copy-start | bytes 1572868
  0.6 70.5 %copy-start.1 = (f32[1,64,2048]{2,1,0:T(8,128)S(1)}, f32[1,64,2048]{2,1,0:T(8,128)}, u32[]{:S(2)}) copy-start(f32[1,64,2048]{2,1,0:T(8,128)} %param.10) | copy-start | bytes 1572868

commit v3 on v2

--- a/solution.py
+++ b/solution.py
@@ -183,13 +183,16 @@
     return pltpu.roll(value, shift % value.shape[axis], axis)
 
 
-def smooth(value, spacing):
-    for axis in (1, 0):
-        value = value + roll(value, spacing, axis)
-        value = value + roll(value, -spacing, axis)
-        value = value + roll(value, spacing, axis)
-        value = value + roll(value, -spacing, axis)
-    return value * (1.0 / 256.0)
+hops = ((2, 2), (1, 1), (3, 3), (1, 3), (3, 1), (2, 1), (1, 2), (2, 3))
+hops = hops + ((3, 2), (2, 0), (0, 2), (1, 0), (0, 1), (3, 0), (0, 3), (0, 0))
+
+
+def others(p):
+    core, x, y = lax.rem(p, 2), lax.rem(p // 2, 4), p // 8
+    for far in (0, 1):
+        for dy, dx in hops:
+            if (dy, dx, far) != (0, 0, 0):
+                yield lax.rem(y + dy, 4) * 8 + lax.rem(x + dx, 4) * 2 + lax.rem(core + far, 2)
 
 
 def drain(ref, sem):
@@ -202,7 +205,7 @@
     shrink_ref, blur_ref,
     est, dirty, psf_wide, row_table, col_table, col_back, row_twist, col_twist, perm,
     psf, abuf, send, recv, spec, send_a, send_b, recv_a, recv_b,
-    hz, hh, hp, hpr, hr, det, energy, ob, mx_own, mx_z, mx_r,
+    hz, hh, hp, hpr, hr, rows_done, smooth_a, smooth_b, det, energy, ob, mx_own, mx_z, mx_r,
     weights, mirror, flipped, mirror_in, in_sems, sems,
 ):
     z = lax.axis_index("chan")
@@ -312,12 +315,8 @@
     partner = remote(flipped, mirror_in, 0, 1, rows=R - 1 - p)
     partner.start()
 
-    def begin(i, carry):
-        to = lax.rem(p + i, R)
+    for to in others(p):
         remote(send.at[to], recv.at[p, 0:TILES], 2, 3, rows=to).start()
-        return carry
-
-    lax.fori_loop(1, R, begin, 0)
     recv[p, 0:TILES] = send[p]
     recv[:, TILES] = jnp.zeros((R, 8, 128), F32)
     for load in loads[5:]:
@@ -332,7 +331,7 @@
     upper = lax.broadcasted_iota(jnp.int32, (8, 128), 0) < 4
     left = lax.broadcasted_iota(jnp.int32, (8, 128), 1) < 64
 
-    def columns(q, carry):
+    def columns(q):
         values = []
         for i in range(R):
             a = recv[i, 2 * q]
@@ -362,22 +361,16 @@
             b = jnp.where(upper, roll(re, 4, 0), im)
             send_a[i, q] = jnp.where(whole, a, roll(b, 64, 1))
             send_b[i, q] = jnp.where(left, roll(a, 64, 1), b)
+
+    def columns_and_send(q, carry):
+        columns(q)
+        for to in others(p):
+            remote(send_a.at[to, q], recv_a.at[p, q], 4, 5, rows=to).start()
         return carry
 
-    lax.fori_loop(0, 3, columns, 0)
-
-    def begin_a(i, carry):
-        to = lax.rem(p + i, R)
-        remote(send_a.at[to], recv_a.at[p], 4, 5, rows=to).start()
-        return carry
-
-    def begin_b(i, carry):
-        to = lax.rem(p + i, R)
+    lax.fori_loop(0, 3, columns_and_send, 0)
+    for to in others(p):
         remote(send_b.at[to, 0:2], recv_b.at[p], 6, 7, rows=to).start()
-        return carry
-
-    lax.fori_loop(1, R, begin_a, 0)
-    lax.fori_loop(1, R, begin_b, 0)
     recv_a[p] = send_a[p]
     recv_b[p] = send_b[p, 0:2]
 
@@ -437,7 +430,7 @@
         abuf[128 * t : 128 * t + 128, :] = dot3(split(block), table, ((0,), (0,)))
     rows_inverse(0, 32, 0, 256)
     pack(0, (0, 3))
-    for i in range(1, Z):
+    for i in (2, 1, 3):
         to = lax.rem(z + i, Z)
         for r in (0, 48):
             rows = slice(r, r + 16)
@@ -452,7 +445,7 @@
         abuf[384 + 128 * t : 512 + 128 * t, :] = dot3(split(block), table, ((0,), (0,)))
     rows_inverse(384, 0, 16, 320)
     pack(1, (1, 2))
-    for i in range(1, Z):
+    for i in (2, 1, 3):
         to = lax.rem(z + i, Z)
         remote(hz.at[to, 16:48], hr.at[z, 32:64, 0:512], 12, 13, chan=to).start()
         remote(hp.at[1, to], hpr.at[1, z], 14, 15, chan=to).start()
@@ -505,23 +498,88 @@
         below.wait_send()
 
 
-    row_ids = lax.broadcasted_iota(jnp.int32, (96, 1), 0) + 64 * p - 16
-    row_mask = jnp.logical_and(row_ids >= 0, row_ids < 64 * R).astype(F32)
-    col_ids = lax.broadcasted_iota(jnp.int32, (1, 640), 1)
-    right_zero = jnp.logical_and(z == Z - 1, jnp.logical_and(col_ids >= 512, col_ids < 576))
-    left_zero = jnp.logical_and(z == 0, col_ids >= 576)
-    col_mask = 1.0 - jnp.logical_or(right_zero, left_zero).astype(F32)
+    lane_8 = lax.broadcasted_iota(jnp.int32, (8, 128), 1)
+    row_8 = lax.broadcasted_iota(jnp.int32, (8, 128), 0)
+    top = jnp.where(p > 0, 1.0, 0.0)
+    bottom = jnp.where(p < R - 1, 1.0, 0.0)
+    side = jnp.where(
+        lane_8 < 64, jnp.where(z < Z - 1, 1.0, 0.0), jnp.where(z > 0, 1.0, 0.0)
+    )
+
+    def down(x, spacing):
+        count = len(x)
+        if spacing == 4:
+            turned = [roll(v, 4, 0) for v in x]
+            mid = [None] + [
+                jnp.where(row_8 < 4, turned[i - 1], turned[i]) for i in range(1, count)
+            ]
+            return [
+                (x[i - 1] + x[i + 1]) * (1 / 256)
+                + (x[i] * (6 / 256) + (mid[i] + mid[i + 1]) * (4 / 256))
+                for i in range(1, count - 1)
+            ]
+        for step in range(4):
+            if step % 2 == 0:
+                turned = [roll(v, spacing, 0) for v in x]
+                x = [x[0] + turned[0]] + [
+                    x[i] + jnp.where(row_8 < spacing, turned[i - 1], turned[i])
+                    for i in range(1, count)
+                ]
+            else:
+                turned = [roll(v, -spacing, 0) for v in x]
+                x = [
+                    x[i] + jnp.where(row_8 >= 8 - spacing, turned[i + 1], turned[i])
+                    for i in range(count - 1)
+                ] + [x[-1] + turned[-1]]
+        return [v * (1 / 256) for v in x]
+
+    def along(x, spacing):
+        for step in range(4):
+            if step % 2 == 0:
+                turned = [roll(v, spacing, 1) for v in x]
+                x = [
+                    x[t] + jnp.where(lane_8 < spacing, turned[t - 1], turned[t]) for t in range(5)
+                ]
+            else:
+                turned = [roll(v, -spacing, 1) for v in x]
+                x = [
+                    x[t] + jnp.where(lane_8 >= 128 - spacing, turned[(t + 1) % 5], turned[t])
+                    for t in range(5)
+                ]
+        return x
 
     def starlet(ch, carry):
-        current = hr[ch]
-        for level in range(3):
-            later = smooth(current, 1 << level)
-            if level < 2:
-                later = later * row_mask * col_mask
-            detail = (current - later)[16:80, 0:512]
-            det[level, ch] = detail
-            energy[level] = energy[level] + detail * detail
-            current = later
+        spans = ((0, 12, 0, 12), (0, 12, 1, 11), (1, 11, 2, 10))
+        for level, (first, last, start, stop) in enumerate(spans):
+            spacing = 1 << level
+            source = (hr.at[ch], smooth_a, smooth_b)[level]
+            target = (smooth_a, smooth_b, None)[level]
+            for t in range(5):
+                lanes = slice(128 * t, 128 * t + 128)
+                x = [source[8 * i : 8 * i + 8, lanes] for i in range(first, last)]
+                for i, value in enumerate(down(x, spacing)):
+                    at = i + (first if spacing < 4 else first + 1)
+                    if start <= at < stop:
+                        rows_done[8 * at : 8 * at + 8, lanes] = value
+            for i in range(start, stop):
+                rows = slice(8 * i, 8 * i + 8)
+                x = [rows_done[rows, 128 * t : 128 * t + 128] for t in range(5)]
+                x = along(x, spacing)
+                if target is not None:
+                    if i < 2:
+                        x = [v * top for v in x]
+                    if i >= 10:
+                        x = [v * bottom for v in x]
+                    x[4] = x[4] * side
+                    for t in range(5):
+                        target[rows, 128 * t : 128 * t + 128] = x[t]
+                if 2 <= i < 10:
+                    at = slice(8 * i - 16, 8 * i - 8)
+                    for t in range(4):
+                        lanes = slice(128 * t, 128 * t + 128)
+                        detail = source[rows, lanes] - x[t]
+                        det[level, ch, at, lanes] = detail
+                        energy[level, at, lanes] = energy[level, at, lanes] + detail * detail
         return carry
 
     energy[...] = jnp.zeros((3, 64, 512), F32)
@@ -562,7 +620,7 @@
     block = pl.ds(pl.multiple_of(512 * z, 512), 512)
 
     def final(i, carry):
-        ch = lax.rem(z + i, Z)
+        ch = lax.rem(z + 2 - (i // 2) + 2 * (i // 3), Z)
         ob[ch] = shrunk(ch)
         remote(ob.at[ch], shrink_ref.at[:, block], 24, 25, chan=ch).start()
         return carry
@@ -595,6 +653,9 @@
         (2, Z, 16, 128),
         (2, Z, 16, 128),
         (Z, 96, 640),
+        (96, 640),
+        (96, 640),
+        (96, 640),
         (3, Z, 64, 512),
         (3, 64, 512),
         (Z, 64, 512),

time: 73.6 us -> 71.8 us (0.976)
  Pallas kernels: 70.5 us -> 68.7 us
    pallas_call x1, Pallas kernels: 70.5 us -> 68.7 us  [shards(): pl.pallas_call(kernel, out_shape=(block, block), in_specs=[anywhere] * le...]
where the time goes in v3:
time: 71.8 us; the launch traced here: 71.7 us
  Pallas kernels  68.7 us (96%)
  other arithmetic  2.3 us (3%)
    pallas_call x1, Pallas kernels, shards(): pl.pallas_call(kernel, out_shape=(block, block), in_specs=[anywhere] * le...  68.7 us
    broadcast_in_dim x1, other arithmetic, shards(): return (new[None], residual[None])  2.3 us

profile of v3, /device:TPU:1, one launch (start us, length us, event | category | flops | bytes accessed | tf_op | source)
XLA Modules:
  0.0 71.7 jit_solution(8206745314656219836)
XLA Ops:
  0.6 0.0 copy-start
  0.6 0.0 copy-start.1
  0.6 68.7 %shard_map.104 = (f32[64,2048]{1,0:T(8,128)}, f32[64,2048]{1,0:T(8,128)}) custom-call(f32[64,2048]{1,0:T(8,128)} %bitcast.12, f32[64,2048]{1,0:T(8,128)} %bitcast.13, f32[64,2048]{1,0:T(8,128)} %bitcast.14, bf16[2,256,256]{2,1,0:T(8,128)(2,1)} %constant.14.clone.row_table_in, bf16[2,256,256]{2,1,0:T(8,128)(2,1)} %constant.15.clone.col_table_in, ...), custom_call_target="tpu_custom_call" | custom-call | tf_op jit(solution)/shard_map/pallas_call | solution.py:670
  69.4 0.0 copy-done
  69.4 0.0 copy-done.1
  69.4 2.3 %subtract_bitcast_fusion.1 = (f32[1,64,2048]{2,1,0:T(8,128)}, f32[1,64,2048]{2,1,0:T(8,128)}) fusion(f32[64,2048]{1,0:T(8,128)} %get-tuple-element.4, f32[1,64,2048]{2,1,0:T(8,128)S(1)} %copy-done.1, f32[64,2048]{1,0:T(8,128)} %get-tuple-element.5, f32[1,64,2048]{2,1,0:T(8,128)S(1)} %copy-done), kind=kLoop, calls=%fused_computation.1 | loop fusion | flops 524288 | bytes 3145728 | tf_op jit(solution)/shard_map/broadcast_in_dim | solution.py:684
Async XLA Ops:
  0.6 68.7 %copy-start = (f32[1,64,2048]{2,1,0:T(8,128)S(1)}, f32[1,64,2048]{2,1,0:T(8,128)}, u32[]{:S(2)}) copy-start(f32[1,64,2048]{2,1,0:T(8,128)} %param.9) | copy-start | bytes 1572868
  0.6 68.7 %copy-start.1 = (f32[1,64,2048]{2,1,0:T(8,128)S(1)}, f32[1,64,2048]{2,1,0:T(8,128)}, u32[]{:S(2)}) copy-start(f32[1,64,2048]{2,1,0:T(8,128)} %param.10) | copy-start | bytes 1572868

commit v4 on v3

--- a/solution.py
+++ b/solution.py
@@ -205,7 +205,7 @@
     shrink_ref, blur_ref,
     est, dirty, psf_wide, row_table, col_table, col_back, row_twist, col_twist, perm,
     psf, abuf, send, recv, spec, send_a, send_b, recv_a, recv_b,
-    hz, hh, hp, hpr, hr, rows_done, smooth_a, smooth_b, det, energy, ob, mx_own, mx_z, mx_r,
+    hz, hh, hp, hpr, hr, smooth_a, smooth_b, det, energy, ob, mx_own, mx_z, mx_r, blur,
     weights, mirror, flipped, mirror_in, in_sems, sems,
 ):
     z = lax.axis_index("chan")
@@ -312,26 +312,25 @@
 
     pl.semaphore_wait(barrier, R - 1 + Z - 1)
 
-    partner = remote(flipped, mirror_in, 0, 1, rows=R - 1 - p)
-    partner.start()
-
     for to in others(p):
         remote(send.at[to], recv.at[p, 0:TILES], 2, 3, rows=to).start()
+
+    def partner(q):
+        return remote(flipped.at[q], mirror_in.at[q], 26 + q, q, rows=R - 1 - p)
+
+    partner(0).start()
+    partner(1).start()
     recv[p, 0:TILES] = send[p]
     recv[:, TILES] = jnp.zeros((R, 8, 128), F32)
     for load in loads[5:]:
         load.wait()
     drain(recv.at[0 : R - 1, 0:TILES], sems.at[3])
     drain(send.at[0 : R - 1], sems.at[2])
-    partner.wait_recv()
-    partner.wait_send()
-    for q in range(2):
-        weights[q] = weights[q] + mirror_in[q]
 
     upper = lax.broadcasted_iota(jnp.int32, (8, 128), 0) < 4
     left = lax.broadcasted_iota(jnp.int32, (8, 128), 1) < 64
 
-    def columns(q):
+    def columns_forward(q):
         values = []
         for i in range(R):
             a = recv[i, 2 * q]
@@ -342,18 +341,21 @@
         for u, (re, im) in enumerate(fft(values, -1)):
             c = col_twist[0, u : u + 1, :]
             s = col_twist[1, u : u + 1, :]
-            spec[8 * u : 8 * u + 8, 0:128] = re * c - im * s
-            spec[8 * u : 8 * u + 8, 128:256] = re * s + im * c
-        out = dot3(split(spec[...]), (col_table[0], col_table[1]), ((1,), (0,)))
-        w = weights[q].reshape(256, 128)
+            spec[q, 8 * u : 8 * u + 8, 0:128] = re * c - im * s
+            spec[q, 8 * u : 8 * u + 8, 128:256] = re * s + im * c
+        spec[q] = dot3(split(spec[q]), (col_table[0], col_table[1]), ((1,), (0,)))
+
+    def columns_inverse(q, w):
+        out = spec[q]
+        w = w.reshape(256, 128)
         out = jnp.concatenate([out[:, 0:128] * w, out[:, 128:256] * w], axis=1)
-        spec[...] = dot3(split(out), (col_back[0], col_back[1]), ((1,), (0,)))
+        spec[q] = dot3(split(out), (col_back[0], col_back[1]), ((1,), (0,)))
         values = []
         for u in range(R):
             c = col_twist[2, u : u + 1, :]
             s = col_twist[3, u : u + 1, :]
-            re = spec[8 * u : 8 * u + 8, 0:128]
-            im = spec[8 * u : 8 * u + 8, 128:256]
+            re = spec[q, 8 * u : 8 * u + 8, 0:128]
+            im = spec[q, 8 * u : 8 * u + 8, 128:256]
             values.append((re * c + im * s, im * c - re * s))
         whole = jnp.logical_or(left, q == 2)
         for i, (re, im) in enumerate(fft(values, 1)):
@@ -362,13 +364,24 @@
             send_a[i, q] = jnp.where(whole, a, roll(b, 64, 1))
             send_b[i, q] = jnp.where(left, roll(a, 64, 1), b)
 
-    def columns_and_send(q, carry):
-        columns(q)
         for to in others(p):
             remote(send_a.at[to, q], recv_a.at[p, q], 4, 5, rows=to).start()
-        return carry
-
-    lax.fori_loop(0, 3, columns_and_send, 0)
+
+    def one_forward(q, carry):
+        columns_forward(q)
+        return carry
+
+    def one_inverse(q, carry):
+        partner(q).wait_recv()
+        columns_inverse(q, weights[q] + mirror_in[q])
+        return carry
+
+    columns_forward(2)
+    columns_inverse(2, weights[2])
+    lax.fori_loop(0, 2, one_forward, 0)
+    lax.fori_loop(0, 2, one_inverse, 0)
+    partner(0).wait_send()
+    partner(1).wait_send()
     for to in others(p):
         remote(send_b.at[to, 0:2], recv_b.at[p], 6, 7, rows=to).start()
     recv_a[p] = send_a[p]
@@ -398,9 +411,9 @@
                 else:
                     blurred = cosine[16 - a] + sine[16 - a]
                 lanes = slice(128 * a, 128 * a + 128)
-                blur_ref[at, lanes] = blurred
+                blur[at, lanes] = blurred
                 halfway = est[at, lanes] + step_size * (dirty[at, lanes] - blurred)
-                hz[a // 4, at, 128 * (a % 4) : 128 * (a % 4) + 128] = halfway
+                hz[a // 4, a % 4, at, :] = halfway
                 if a % 4 in (0, 3):
                     edges[a] = halfway
             none = jnp.zeros((8, 128), F32)
@@ -422,7 +435,7 @@
     def unpack(half, groups):
         for c in range(Z):
             for e, g in enumerate(groups):
-                hr[c, 16 + 16 * g : 32 + 16 * g, 512:640] = roll(hpr[half, c], -32 * e - 16, 1)
+                hr[c, 4, 24 + 16 * g : 40 + 16 * g, :] = roll(hpr[half, c], -32 * e - 16, 1)
 
     drain(recv_a.at[0 : R - 1], sems.at[5])
     for t in range(3):
@@ -433,9 +446,8 @@
     for i in (2, 1, 3):
         to = lax.rem(z + i, Z)
         for r in (0, 48):
-            rows = slice(r, r + 16)
             remote(
-                hz.at[to, rows], hr.at[z, r + 16 : r + 32, 0:512], 8, 9, chan=to
+                hz.at[to, :, r : r + 16], hr.at[z, 0:4, r + 24 : r + 40], 8, 9, chan=to
             ).start()
         remote(hp.at[0, to], hpr.at[0, z], 10, 11, chan=to).start()
 
@@ -445,28 +457,33 @@
         abuf[384 + 128 * t : 512 + 128 * t, :] = dot3(split(block), table, ((0,), (0,)))
     rows_inverse(384, 0, 16, 320)
     pack(1, (1, 2))
+    blur_out = pltpu.make_async_copy(blur, blur_ref, sems.at[29])
+    blur_out.start()
     for i in (2, 1, 3):
         to = lax.rem(z + i, Z)
-        remote(hz.at[to, 16:48], hr.at[z, 32:64, 0:512], 12, 13, chan=to).start()
+        remote(hz.at[to, :, 16:48], hr.at[z, 0:4, 40:72], 12, 13, chan=to).start()
         remote(hp.at[1, to], hpr.at[1, z], 14, 15, chan=to).start()
     drain(send_a.at[0 : R - 1], sems.at[4])
     drain(send_b.at[0 : R - 1, 0:2], sems.at[6])
-    hr[z, 16:80, 0:512] = hz[z]
+    hr[z, 0:4, 24:88] = hz[z]
     hpr[:, z] = hp[:, z]
+
+    hr[:, :, 0:8, :] = jnp.zeros((Z, 5, 8, 128), F32)
+    hr[:, :, 104:112, :] = jnp.zeros((Z, 5, 8, 128), F32)
 
     @pl.when(p == 0)
     def _():
-        hr[:, 0:16, :] = jnp.zeros((Z, 16, 640), F32)
+        hr[:, :, 8:24, :] = jnp.zeros((Z, 5, 16, 128), F32)
 
     @pl.when(p == R - 1)
     def _():
-        hr[:, 80:96, :] = jnp.zeros((Z, 16, 640), F32)
-
-    drain(hz.at[0 : Z - 1, 0:32], sems.at[9])
+        hr[:, :, 88:104, :] = jnp.zeros((Z, 5, 16, 128), F32)
+
+    drain(hz.at[0 : Z - 1, :, 0:32], sems.at[9])
     drain(hp.at[0, 0 : Z - 1], sems.at[11])
     unpack(0, (0, 3))
-    above = remote(hr.at[:, 16:32, :], hr.at[:, 80:96, :], 16, 17, rows=lax.rem(p + R - 1, R))
-    below = remote(hr.at[:, 64:80, :], hr.at[:, 0:16, :], 18, 19, rows=lax.rem(p + 1, R))
+    above = remote(hr.at[:, :, 24:40], hr.at[:, :, 88:104], 16, 17, rows=lax.rem(p + R - 1, R))
+    below = remote(hr.at[:, :, 72:88], hr.at[:, :, 8:24], 18, 19, rows=lax.rem(p + 1, R))
 
     @pl.when(p > 0)
     def _():
@@ -476,12 +493,12 @@
     def _():
         below.start()
 
-    drain(hz.at[0 : Z - 1, 0:32], sems.at[13])
+    drain(hz.at[0 : Z - 1, :, 0:32], sems.at[13])
     drain(hp.at[0, 0 : Z - 1], sems.at[15])
     unpack(1, (1, 2))
-    drain(hz.at[0 : Z - 1, 0:32], sems.at[8])
+    drain(hz.at[0 : Z - 1, :, 0:32], sems.at[8])
     drain(hp.at[0, 0 : Z - 1], sems.at[10])
-    drain(hz.at[0 : Z - 1, 0:32], sems.at[12])
+    drain(hz.at[0 : Z - 1, :, 0:32], sems.at[12])
     drain(hp.at[0, 0 : Z - 1], sems.at[14])
 
     @pl.when(p < R - 1)
@@ -499,39 +516,16 @@
 
 
     lane_8 = lax.broadcasted_iota(jnp.int32, (8, 128), 1)
-    row_8 = lax.broadcasted_iota(jnp.int32, (8, 128), 0)
     top = jnp.where(p > 0, 1.0, 0.0)
     bottom = jnp.where(p < R - 1, 1.0, 0.0)
     side = jnp.where(
         lane_8 < 64, jnp.where(z < Z - 1, 1.0, 0.0), jnp.where(z > 0, 1.0, 0.0)
     )
 
-    def down(x, spacing):
-        count = len(x)
-        if spacing == 4:
-            turned = [roll(v, 4, 0) for v in x]
-            mid = [None] + [
-                jnp.where(row_8 < 4, turned[i - 1], turned[i]) for i in range(1, count)
-            ]
-            return [
-                (x[i - 1] + x[i + 1]) * (1 / 256)
-                + (x[i] * (6 / 256) + (mid[i] + mid[i + 1]) * (4 / 256))
-                for i in range(1, count - 1)
-            ]
-        for step in range(4):
-            if step % 2 == 0:
-                turned = [roll(v, spacing, 0) for v in x]
-                x = [x[0] + turned[0]] + [
-                    x[i] + jnp.where(row_8 < spacing, turned[i - 1], turned[i])
-                    for i in range(1, count)
-                ]
-            else:
-                turned = [roll(v, -spacing, 0) for v in x]
-                x = [
-                    x[i] + jnp.where(row_8 >= 8 - spacing, turned[i + 1], turned[i])
-                    for i in range(count - 1)
-                ] + [x[-1] + turned[-1]]
-        return [v * (1 / 256) for v in x]
+    def down(source, t, row, spacing):
+        x = [source[t, row + k * spacing : row + k * spacing + 8, :] for k in range(-2, 3)]
+        near, far = x[1] + x[3], x[0] + x[4]
+        return far * (1 / 256) + (x[2] * (6 / 256) + near * (4 / 256))
 
     def along(x, spacing):
         for step in range(4):
@@ -549,22 +543,12 @@
         return x
 
     def starlet(ch, carry):
-        spans = ((0, 12, 0, 12), (0, 12, 1, 11), (1, 11, 2, 10))
-        for level, (first, last, start, stop) in enumerate(spans):
-            spacing = 1 << level
+        for level, (start, stop) in enumerate(((0, 12), (1, 11), (2, 10))):
             source = (hr.at[ch], smooth_a, smooth_b)[level]
             target = (smooth_a, smooth_b, None)[level]
-            for t in range(5):
-                lanes = slice(128 * t, 128 * t + 128)
-                x = [source[8 * i : 8 * i + 8, lanes] for i in range(first, last)]
-                for i, value in enumerate(down(x, spacing)):
-                    at = i + (first if spacing < 4 else first + 1)
-                    if start <= at < stop:
-                        rows_done[8 * at : 8 * at + 8, lanes] = value
             for i in range(start, stop):
-                rows = slice(8 * i, 8 * i + 8)
-                x = [rows_done[rows, 128 * t : 128 * t + 128] for t in range(5)]
-                x = along(x, spacing)
+                rows = slice(8 * i + 8, 8 * i + 16)
+                x = along([down(source, t, 8 * i + 8, 1 << level) for t in range(5)], 1 << level)
                 if target is not None:
                     if i < 2:
                         x = [v * top for v in x]
@@ -572,23 +556,25 @@
                         x = [v * bottom for v in x]
                     x[4] = x[4] * side
                     for t in range(5):
-                        target[rows, 128 * t : 128 * t + 128] = x[t]
+                        target[t, rows, :] = x[t]
                 if 2 <= i < 10:
                     at = slice(8 * i - 16, 8 * i - 8)
                     for t in range(4):
-                        lanes = slice(128 * t, 128 * t + 128)
-                        detail = source[rows, lanes] - x[t]
-                        det[level, ch, at, lanes] = detail
-                        energy[level, at, lanes] = energy[level, at, lanes] + detail * detail
-        return carry
-
-    energy[...] = jnp.zeros((3, 64, 512), F32)
+                        detail = source[t, rows, :] - x[t]
+                        det[level, ch, t, at, :] = detail
+                        energy[level, t, at, :] = energy[level, t, at, :] + detail * detail
+        return carry
+
+    energy[...] = jnp.zeros((3, 4, 64, 128), F32)
     lax.fori_loop(0, Z, starlet, 0)
 
-    lane = lax.broadcasted_iota(jnp.int32, (1, 128), 1)
-    peaks = jnp.zeros((1, 128), F32)
-    for level in range(3):
-        peaks = jnp.where(lane == level, jnp.max(energy[level]), peaks)
+    peaks = jnp.concatenate(
+        [
+            jnp.max(jnp.max(energy[level], axis=0), axis=0, keepdims=True)
+            for level in range(3)
+        ],
+        axis=1,
+    )
     mx_own[0] = peaks
     for i in range(1, Z):
         remote(mx_own.at[0], mx_z.at[z], 20, 21, chan=lax.rem(z + i, Z)).start()
@@ -609,33 +595,37 @@
     drain(mx_z.at[0 : Z - 1], sems.at[20])
     peaks = jnp.sqrt(jnp.max(mx_r[...], axis=0))
     for level in range(3):
-        threshold = fractions[level] * jnp.max(jnp.where(lane == level, peaks, 0.0))
-        energy[level] = jnp.minimum(energy[level] * threshold, 1.0)
+        peak = jnp.max(peaks[:, 128 * level : 128 * level + 128], axis=1, keepdims=True)
+        energy[level] = jnp.minimum(energy[level] * (fractions[level] * peak), 1.0)
 
     def shrunk(ch):
-        out = energy[0] * det[0, ch]
-        out = out + energy[1] * det[1, ch]
-        return out + energy[2] * det[2, ch]
+        for t in range(4):
+            out = energy[0, t] * det[0, ch, t]
+            out = out + energy[1, t] * det[1, ch, t]
+            ob[ch, :, 128 * t : 128 * t + 128] = out + energy[2, t] * det[2, ch, t]
 
     block = pl.ds(pl.multiple_of(512 * z, 512), 512)
 
     def final(i, carry):
         ch = lax.rem(z + 2 - (i // 2) + 2 * (i // 3), Z)
-        ob[ch] = shrunk(ch)
+        shrunk(ch)
         remote(ob.at[ch], shrink_ref.at[:, block], 24, 25, chan=ch).start()
         return carry
 
     lax.fori_loop(1, Z, final, 0)
-    shrink_ref[:, block] = shrunk(z)
+    shrunk(z)
+    own = pltpu.make_async_copy(ob.at[z], shrink_ref.at[:, block], sems.at[28])
+    own.start()
     drain(ob.at[0 : Z - 1], sems.at[25])
     drain(ob.at[0 : Z - 1], sems.at[24])
+    own.wait()
+    blur_out.wait()
 
 
 def shards(estimate, dirty_image, psf_weights):
     constants = tables()
     arguments = (estimate[0], dirty_image[0], psf_weights[0].T, *constants)
     anywhere = pl.BlockSpec(memory_space=pl.ANY)
-    vmem = pl.BlockSpec(memory_space=pltpu.VMEM)
     block = jax.ShapeDtypeStruct((64, 2048), F32)
     dma = pltpu.SemaphoreType.DMA
     shapes = [
@@ -643,25 +633,25 @@
         (640, 256),
         (R, TILES, 8, 128),
         (R, TILES + 1, 8, 128),
-        (256, 256),
+        (3, 256, 256),
         (R, 3, 8, 128),
         (R, 3, 8, 128),
         (R, 3, 8, 128),
         (R, 2, 8, 128),
-        (Z, 64, 512),
+        (Z, 4, 64, 128),
         (Z, 64, 128),
         (2, Z, 16, 128),
         (2, Z, 16, 128),
-        (Z, 96, 640),
-        (96, 640),
-        (96, 640),
-        (96, 640),
-        (3, Z, 64, 512),
-        (3, 64, 512),
+        (Z, 5, 112, 128),
+        (5, 112, 128),
+        (5, 112, 128),
+        (3, Z, 4, 64, 128),
+        (3, 4, 64, 128),
         (Z, 64, 512),
-        (2, 1, 128),
-        (Z, 1, 128),
-        (R, 1, 128),
+        (2, 1, 384),
+        (Z, 1, 384),
+        (R, 1, 384),
+        (64, 2048),
         (3, 32, 8, 128),
         (2, 32, 8, 128),
         (2, 32, 8, 128),
@@ -671,10 +661,10 @@
         kernel,
         out_shape=(block, block),
         in_specs=[anywhere] * len(arguments),
-        out_specs=(vmem, vmem),
+        out_specs=(anywhere, anywhere),
         scratch_shapes=[pltpu.VMEM(a.shape, a.dtype) for a in arguments]
         + [pltpu.VMEM(shape, F32) for shape in shapes]
-        + [dma((len(arguments),)), dma((26,))],
+        + [dma((len(arguments),)), dma((30,))],
         compiler_params=pltpu.CompilerParams(
             collective_id=0, has_side_effects=True, vmem_limit_bytes=VMEM_LIMIT
         ),

time: 71.8 us -> 69.3 us (0.965)
  Pallas kernels: 68.7 us -> 66.2 us
    pallas_call x1, Pallas kernels: 68.7 us -> 66.2 us  [shards(): pl.pallas_call(kernel, out_shape=(block, block), in_specs=[anywhere] * le...]
where the time goes in v4:
time: 69.3 us; the launch traced here: 69.2 us
  Pallas kernels  66.2 us (96%)
  other arithmetic  2.3 us (3%)
    pallas_call x1, Pallas kernels, shards(): pl.pallas_call(kernel, out_shape=(block, block), in_specs=[anywhere] * le...  66.2 us
    broadcast_in_dim x1, other arithmetic, shards(): return (new[None], residual[None])  2.3 us

profile of v4, /device:TPU:1, one launch (start us, length us, event | category | flops | bytes accessed | tf_op | source)
XLA Modules:
  0.0 69.2 jit_solution(6752190036510108921)
XLA Ops:
  0.6 0.0 copy-start
  0.6 0.0 copy-start.1
  0.6 66.2 %shard_map.104 = (f32[64,2048]{1,0:T(8,128)}, f32[64,2048]{1,0:T(8,128)}) custom-call(f32[64,2048]{1,0:T(8,128)} %bitcast.12, f32[64,2048]{1,0:T(8,128)} %bitcast.13, f32[64,2048]{1,0:T(8,128)} %bitcast.14, bf16[2,256,256]{2,1,0:T(8,128)(2,1)} %constant.14.clone.row_table_in, bf16[2,256,256]{2,1,0:T(8,128)(2,1)} %constant.15.clone.col_table_in, ...), custom_call_target="tpu_custom_call" | custom-call | tf_op jit(solution)/shard_map/pallas_call | solution.py:660
  66.9 0.0 copy-done
  66.9 0.0 copy-done.1
  66.9 2.3 %subtract_bitcast_fusion.1 = (f32[1,64,2048]{2,1,0:T(8,128)}, f32[1,64,2048]{2,1,0:T(8,128)}) fusion(f32[64,2048]{1,0:T(8,128)} %get-tuple-element.4, f32[1,64,2048]{2,1,0:T(8,128)S(1)} %copy-done.1, f32[64,2048]{1,0:T(8,128)} %get-tuple-element.5, f32[1,64,2048]{2,1,0:T(8,128)S(1)} %copy-done), kind=kLoop, calls=%fused_computation.1 | loop fusion | flops 524288 | bytes 3145728 | tf_op jit(solution)/shard_map/broadcast_in_dim | solution.py:674
Async XLA Ops:
  0.6 66.2 %copy-start = (f32[1,64,2048]{2,1,0:T(8,128)S(1)}, f32[1,64,2048]{2,1,0:T(8,128)}, u32[]{:S(2)}) copy-start(f32[1,64,2048]{2,1,0:T(8,128)} %param.9) | copy-start | bytes 1572868
  0.6 66.2 %copy-start.1 = (f32[1,64,2048]{2,1,0:T(8,128)S(1)}, f32[1,64,2048]{2,1,0:T(8,128)}, u32[]{:S(2)}) copy-start(f32[1,64,2048]{2,1,0:T(8,128)} %param.10) | copy-start | bytes 1572868

commit v5 on v4

--- a/solution.py
+++ b/solution.py
@@ -205,7 +205,7 @@
     shrink_ref, blur_ref,
     est, dirty, psf_wide, row_table, col_table, col_back, row_twist, col_twist, perm,
     psf, abuf, send, recv, spec, send_a, send_b, recv_a, recv_b,
-    hz, hh, hp, hpr, hr, smooth_a, smooth_b, det, energy, ob, mx_own, mx_z, mx_r, blur,
+    hz, hh, hp, hpr, hr, rows_done, smooth_a, smooth_b, det, energy, ob, mx_own, mx_z, mx_r, blur,
     weights, mirror, flipped, mirror_in, in_sems, sems,
 ):
     z = lax.axis_index("chan")
@@ -522,33 +522,79 @@
         lane_8 < 64, jnp.where(z < Z - 1, 1.0, 0.0), jnp.where(z > 0, 1.0, 0.0)
     )
 
-    def down(source, t, row, spacing):
-        x = [source[t, row + k * spacing : row + k * spacing + 8, :] for k in range(-2, 3)]
-        near, far = x[1] + x[3], x[0] + x[4]
-        return far * (1 / 256) + (x[2] * (6 / 256) + near * (4 / 256))
-
-    def along(x, spacing):
-        for step in range(4):
-            if step % 2 == 0:
-                turned = [roll(v, spacing, 1) for v in x]
-                x = [
-                    x[t] + jnp.where(lane_8 < spacing, turned[t - 1], turned[t]) for t in range(5)
+    row_8 = lax.broadcasted_iota(jnp.int32, (8, 128), 0)
+
+    def down(x, spacing):
+        count = len(x)
+        half = [roll(v, 4, 0) for v in x] if spacing > 1 else None
+        if spacing > 1:
+            half = (
+                [half[0]]
+                + [jnp.where(row_8 < 4, half[i - 1], half[i]) for i in range(1, count)]
+                + [half[-1]]
+            )
+        if spacing == 4:
+            return [None] + [
+                (x[i - 1] + x[i + 1]) * (1 / 256)
+                + (x[i] * (6 / 256) + (half[i] + half[i + 1]) * (4 / 256))
+                for i in range(1, count - 1)
+            ]
+        if spacing == 2:
+            plus = [roll(v, 2, 0) for v in x]
+            minus = [roll(v, -2, 0) for v in x]
+            out = []
+            for i in range(count):
+                above = jnp.where(row_8 < 2, plus[max(i - 1, 0)], plus[i])
+                below = jnp.where(row_8 >= 6, minus[min(i + 1, count - 1)], minus[i])
+                out.append(
+                    (half[i] + half[i + 1]) * (1 / 256)
+                    + (x[i] * (6 / 256) + (above + below) * (4 / 256))
+                )
+            return out
+        shifted = {}
+        for k in (1, -1, 2, -2):
+            turned = [roll(v, k, 0) for v in x]
+            if k > 0:
+                shifted[k] = [
+                    jnp.where(row_8 < k, turned[max(i - 1, 0)], turned[i]) for i in range(count)
                 ]
             else:
-                turned = [roll(v, -spacing, 1) for v in x]
-                x = [
-                    x[t] + jnp.where(lane_8 >= 128 - spacing, turned[(t + 1) % 5], turned[t])
-                    for t in range(5)
+                shifted[k] = [
+                    jnp.where(row_8 >= 8 + k, turned[min(i + 1, count - 1)], turned[i])
+                    for i in range(count)
                 ]
-        return x
+        return [
+            (shifted[2][i] + shifted[-2][i]) * (1 / 256)
+            + (x[i] * (6 / 256) + (shifted[1][i] + shifted[-1][i]) * (4 / 256))
+            for i in range(count)
+        ]
+
+    def along(x, spacing):
+        total = []
+        rolled = {k: [roll(v, k * spacing, 1) for v in x] for k in (1, -1, 2, -2)}
+        for t in range(5):
+            near = jnp.where(lane_8 < spacing, rolled[1][t - 1], rolled[1][t]) + jnp.where(
+                lane_8 >= 128 - spacing, rolled[-1][(t + 1) % 5], rolled[-1][t]
+            )
+            far = jnp.where(lane_8 < 2 * spacing, rolled[2][t - 1], rolled[2][t]) + jnp.where(
+                lane_8 >= 128 - 2 * spacing, rolled[-2][(t + 1) % 5], rolled[-2][t]
+            )
+            total.append(6.0 * x[t] + (4.0 * near + far))
+        return total
 
     def starlet(ch, carry):
         for level, (start, stop) in enumerate(((0, 12), (1, 11), (2, 10))):
             source = (hr.at[ch], smooth_a, smooth_b)[level]
             target = (smooth_a, smooth_b, None)[level]
+            first, last = ((0, 12), (0, 12), (1, 11))[level]
+            for t in range(5):
+                x = [source[t, 8 * i + 8 : 8 * i + 16, :] for i in range(first, last)]
+                x = down(x, 1 << level)
+                for i in range(start, stop):
+                    rows_done[t, 8 * i + 8 : 8 * i + 16, :] = x[i - first]
             for i in range(start, stop):
                 rows = slice(8 * i + 8, 8 * i + 16)
-                x = along([down(source, t, 8 * i + 8, 1 << level) for t in range(5)], 1 << level)
+                x = along([rows_done[t, rows, :] for t in range(5)], 1 << level)
                 if target is not None:
                     if i < 2:
                         x = [v * top for v in x]
@@ -643,6 +689,7 @@
         (2, Z, 16, 128),
         (2, Z, 16, 128),
         (Z, 5, 112, 128),
+        (5, 112, 128),
         (5, 112, 128),
         (5, 112, 128),
         (3, Z, 4, 64, 128),

time: 69.3 us -> 66.1 us (0.954)
  Pallas kernels: 66.2 us -> 63 us
    pallas_call x1, Pallas kernels: 66.2 us -> 63 us  [shards(): pl.pallas_call(kernel, out_shape=(block, block), in_specs=[anywhere] * le...]
where the time goes in v5:
time: 66.1 us; the launch traced here: 66 us
  Pallas kernels  63 us (95%)
  other arithmetic  2.3 us (3%)
  between operations  0.67 us (1%)
    pallas_call x1, Pallas kernels, shards(): pl.pallas_call(kernel, out_shape=(block, block), in_specs=[anywhere] * le...  63 us
    broadcast_in_dim x1, other arithmetic, shards(): return (new[None], residual[None])  2.3 us

profile of v5, /device:TPU:1, one launch (start us, length us, event | category | flops | bytes accessed | tf_op | source)
XLA Modules:
  0.0 66.0 jit_solution(2155508396726681906)
XLA Ops:
  0.6 0.0 copy-start
  0.6 0.0 copy-start.1
  0.6 63.0 %shard_map.104 = (f32[64,2048]{1,0:T(8,128)}, f32[64,2048]{1,0:T(8,128)}) custom-call(f32[64,2048]{1,0:T(8,128)} %bitcast.12, f32[64,2048]{1,0:T(8,128)} %bitcast.13, f32[64,2048]{1,0:T(8,128)} %bitcast.14, bf16[2,256,256]{2,1,0:T(8,128)(2,1)} %constant.14.clone.row_table_in, bf16[2,256,256]{2,1,0:T(8,128)(2,1)} %constant.15.clone.col_table_in, ...), custom_call_target="tpu_custom_call" | custom-call | tf_op jit(solution)/shard_map/pallas_call | solution.py:707
  63.7 0.0 copy-done
  63.7 0.0 copy-done.1
  63.7 2.3 %subtract_bitcast_fusion.1 = (f32[1,64,2048]{2,1,0:T(8,128)}, f32[1,64,2048]{2,1,0:T(8,128)}) fusion(f32[64,2048]{1,0:T(8,128)} %get-tuple-element.4, f32[1,64,2048]{2,1,0:T(8,128)S(1)} %copy-done.1, f32[64,2048]{1,0:T(8,128)} %get-tuple-element.5, f32[1,64,2048]{2,1,0:T(8,128)S(1)} %copy-done), kind=kLoop, calls=%fused_computation.1 | loop fusion | flops 524288 | bytes 3145728 | tf_op jit(solution)/shard_map/broadcast_in_dim | solution.py:721
Async XLA Ops:
  0.6 63.0 %copy-start = (f32[1,64,2048]{2,1,0:T(8,128)S(1)}, f32[1,64,2048]{2,1,0:T(8,128)}, u32[]{:S(2)}) copy-start(f32[1,64,2048]{2,1,0:T(8,128)} %param.9) | copy-start | bytes 1572868
  0.6 63.0 %copy-start.1 = (f32[1,64,2048]{2,1,0:T(8,128)S(1)}, f32[1,64,2048]{2,1,0:T(8,128)}, u32[]{:S(2)}) copy-start(f32[1,64,2048]{2,1,0:T(8,128)} %param.10) | copy-start | bytes 1572868

commit v6 on v5

--- a/solution.py
+++ b/solution.py
@@ -17,7 +17,7 @@
 R = 32
 Z = 4
 VMEM_LIMIT = 60 * 1024 * 1024
-TILES = 5
+TILES = 4
 
 
 def linear(pairs):
@@ -169,7 +169,9 @@
         high = table.astype(BF16)
         return np.stack([high, (table - high.astype(np.float64)).astype(BF16)])
 
+    real = rows[:, 0:128].reshape(32, 2, 4, 128).transpose(1, 0, 2, 3).reshape(256, 128)
     return (
+        halves(real),
         halves(rows),
         halves(cols),
         halves(back),
@@ -200,11 +202,11 @@
 
 
 def kernel(
-    est_in, dirty_in, psf_in, row_table_in, col_table_in, col_back_in, row_twist_in, col_twist_in,
+    est_in, dirty_in, psf_in, real_table_in, row_table_in, col_table_in, col_back_in, row_twist_in, col_twist_in,
     perm_in,
     shrink_ref, blur_ref,
-    est, dirty, psf_wide, row_table, col_table, col_back, row_twist, col_twist, perm,
-    psf, abuf, send, recv, spec, send_a, send_b, recv_a, recv_b,
+    est, dirty, psf_wide, real_table, row_table, col_table, col_back, row_twist, col_twist, perm,
+    psf, abuf, send, recv, send_8, recv_8, spec, send_a, send_b, recv_a, recv_b, send_9, recv_9,
     hz, hh, hp, hpr, hr, rows_done, smooth_a, smooth_b, det, energy, ob, mx_own, mx_z, mx_r, blur,
     weights, mirror, flipped, mirror_in, in_sems, sems,
 ):
@@ -231,7 +233,7 @@
     pairs = (
         (est_in, est), (row_twist_in, row_twist), (row_table_in, row_table), (psf_in, psf_wide),
         (perm_in, perm), (col_twist_in, col_twist), (col_table_in, col_table),
-        (col_back_in, col_back), (dirty_in, dirty),
+        (col_back_in, col_back), (dirty_in, dirty), (real_table_in, real_table),
     )
     loads = [pltpu.make_async_copy(a, b, in_sems.at[i]) for i, (a, b) in enumerate(pairs)]
     for load in loads:
@@ -248,6 +250,7 @@
         )
 
     abuf[576:640, :] = jnp.zeros((64, 256), F32)
+    left = lax.broadcasted_iota(jnp.int32, (8, 128), 1) < 64
     for load in loads[:3]:
         load.wait()
 
@@ -278,6 +281,11 @@
     for t in range(TILES):
         out = dot3(table, split(abuf[128 * t : 128 * t + 128, :]), ((1,), (1,)))
         send[:, t] = out.reshape(R, 8, 128)
+    out = dot3(table, split(abuf[512:640, :]), ((1,), (1,)))
+    for i in range(R):
+        value = out[8 * i : 8 * i + 8]
+        value = jnp.where(left, value, roll(roll(value, 64, 1), 4, 0))
+        send_8[i] = value[0:4]
 
     left_half = lax.broadcasted_iota(jnp.int32, (40, 128), 1) < 64
     for load in loads[3:5]:
@@ -313,32 +321,39 @@
     pl.semaphore_wait(barrier, R - 1 + Z - 1)
 
     for to in others(p):
-        remote(send.at[to], recv.at[p, 0:TILES], 2, 3, rows=to).start()
+        remote(send.at[to], recv.at[p], 2, 3, rows=to).start()
+    for to in others(p):
+        remote(send_8.at[to], recv_8.at[p], 30, 31, rows=to).start()
 
     def partner(q):
         return remote(flipped.at[q], mirror_in.at[q], 26 + q, q, rows=R - 1 - p)
 
     partner(0).start()
     partner(1).start()
-    recv[p, 0:TILES] = send[p]
-    recv[:, TILES] = jnp.zeros((R, 8, 128), F32)
+    recv[p] = send[p]
+    recv_8[p] = send_8[p]
     for load in loads[5:]:
         load.wait()
-    drain(recv.at[0 : R - 1, 0:TILES], sems.at[3])
-    drain(send.at[0 : R - 1], sems.at[2])
+    drain(recv_8.at[0 : R - 1], sems.at[31])
+    drain(recv.at[0 : R - 1], sems.at[3])
 
     upper = lax.broadcasted_iota(jnp.int32, (8, 128), 0) < 4
-    left = lax.broadcasted_iota(jnp.int32, (8, 128), 1) < 64
-
-    def columns_forward(q):
-        values = []
+    even = lax.broadcasted_iota(jnp.int32, (8, 128), 1) // 32 % 2 == 0
+
+    def gathered(q):
         for i in range(R):
             a = recv[i, 2 * q]
             b = recv[i, 2 * q + 1]
-            values.append(
-                (jnp.where(upper, a, roll(b, 4, 0)), jnp.where(upper, roll(a, 4, 0), b))
-            )
-        for u, (re, im) in enumerate(fft(values, -1)):
+            yield (jnp.where(upper, a, roll(b, 4, 0)), jnp.where(upper, roll(a, 4, 0), b))
+
+    def gathered_8():
+        none = jnp.zeros((4, 128), F32)
+        for i in range(R):
+            a = jnp.concatenate([recv_8[i], none], axis=0)
+            yield (jnp.where(left, a, 0.0), jnp.where(left, roll(a, 64, 1), 0.0))
+
+    def columns_forward(q, values):
+        for u, (re, im) in enumerate(fft(list(values), -1)):
             c = col_twist[0, u : u + 1, :]
             s = col_twist[1, u : u + 1, :]
             spec[q, 8 * u : 8 * u + 8, 0:128] = re * c - im * s
@@ -357,35 +372,35 @@
             re = spec[q, 8 * u : 8 * u + 8, 0:128]
             im = spec[q, 8 * u : 8 * u + 8, 128:256]
             values.append((re * c + im * s, im * c - re * s))
-        whole = jnp.logical_or(left, q == 2)
-        for i, (re, im) in enumerate(fft(values, 1)):
+        return fft(values, 1)
+
+    def one_forward(q, carry):
+        columns_forward(q, gathered(q))
+        return carry
+
+    def one_inverse(q, carry):
+        partner(q).wait_recv()
+        for i, (re, im) in enumerate(columns_inverse(q, weights[q] + mirror_in[q])):
             a = jnp.where(upper, re, roll(im, 4, 0))
             b = jnp.where(upper, roll(re, 4, 0), im)
-            send_a[i, q] = jnp.where(whole, a, roll(b, 64, 1))
+            send_a[i, q] = jnp.where(left, a, roll(b, 64, 1))
             send_b[i, q] = jnp.where(left, roll(a, 64, 1), b)
-
         for to in others(p):
             remote(send_a.at[to, q], recv_a.at[p, q], 4, 5, rows=to).start()
-
-    def one_forward(q, carry):
-        columns_forward(q)
         return carry
 
-    def one_inverse(q, carry):
-        partner(q).wait_recv()
-        columns_inverse(q, weights[q] + mirror_in[q])
-        return carry
-
-    columns_forward(2)
-    columns_inverse(2, weights[2])
+    columns_forward(2, gathered_8())
+    for i, (re, im) in enumerate(columns_inverse(2, weights[2])):
+        send_9[i] = jnp.where(even, re, roll(im, 32, 1))[0:4]
+    for to in others(p):
+        remote(send_9.at[to], recv_9.at[p], 32, 33, rows=to).start()
     lax.fori_loop(0, 2, one_forward, 0)
     lax.fori_loop(0, 2, one_inverse, 0)
-    partner(0).wait_send()
-    partner(1).wait_send()
     for to in others(p):
-        remote(send_b.at[to, 0:2], recv_b.at[p], 6, 7, rows=to).start()
+        remote(send_b.at[to], recv_b.at[p], 6, 7, rows=to).start()
     recv_a[p] = send_a[p]
-    recv_b[p] = send_b[p, 0:2]
+    recv_b[p] = send_b[p]
+    recv_9[p] = send_9[p]
 
     def rows_inverse(base, spread, first, last):
         def group(g, carry):
@@ -438,7 +453,15 @@
                 hr[c, 4, 24 + 16 * g : 40 + 16 * g, :] = roll(hpr[half, c], -32 * e - 16, 1)
 
     drain(recv_a.at[0 : R - 1], sems.at[5])
-    for t in range(3):
+    drain(recv_9.at[0 : R - 1], sems.at[33])
+    block = split(recv_9[...].reshape(128, 128))
+    real, imag = (
+        dot3(block, (real_table[0, at : at + 128], real_table[1, at : at + 128]), ((0,), (0,)))
+        for at in (0, 128)
+    )
+    abuf[256:288, 0:128] = real[0:32] + imag[32:64]
+    abuf[320:352, 0:128] = real[64:96] + imag[96:128]
+    for t in range(2):
         block = recv_a[:, t].reshape(256, 128)
         abuf[128 * t : 128 * t + 128, :] = dot3(split(block), table, ((0,), (0,)))
     rows_inverse(0, 32, 0, 256)
@@ -463,8 +486,6 @@
         to = lax.rem(z + i, Z)
         remote(hz.at[to, :, 16:48], hr.at[z, 0:4, 40:72], 12, 13, chan=to).start()
         remote(hp.at[1, to], hpr.at[1, z], 14, 15, chan=to).start()
-    drain(send_a.at[0 : R - 1], sems.at[4])
-    drain(send_b.at[0 : R - 1, 0:2], sems.at[6])
     hr[z, 0:4, 24:88] = hz[z]
     hpr[:, z] = hp[:, z]
 
@@ -496,10 +517,6 @@
     drain(hz.at[0 : Z - 1, :, 0:32], sems.at[13])
     drain(hp.at[0, 0 : Z - 1], sems.at[15])
     unpack(1, (1, 2))
-    drain(hz.at[0 : Z - 1, :, 0:32], sems.at[8])
-    drain(hp.at[0, 0 : Z - 1], sems.at[10])
-    drain(hz.at[0 : Z - 1, :, 0:32], sems.at[12])
-    drain(hp.at[0, 0 : Z - 1], sems.at[14])
 
     @pl.when(p < R - 1)
     def _():
@@ -508,11 +525,6 @@
     @pl.when(p > 0)
     def _():
         below.wait_recv()
-        above.wait_send()
-
-    @pl.when(p < R - 1)
-    def _():
-        below.wait_send()
 
 
     lane_8 = lax.broadcasted_iota(jnp.int32, (8, 128), 1)
@@ -637,8 +649,6 @@
     mx_r[p] = peaks
     energy[...] = lax.rsqrt(energy[...])
     drain(mx_r.at[0 : R - 1], sems.at[23])
-    drain(mx_r.at[0 : R - 1], sems.at[22])
-    drain(mx_z.at[0 : Z - 1], sems.at[20])
     peaks = jnp.sqrt(jnp.max(mx_r[...], axis=0))
     for level in range(3):
         peak = jnp.max(peaks[:, 128 * level : 128 * level + 128], axis=1, keepdims=True)
@@ -662,6 +672,28 @@
     shrunk(z)
     own = pltpu.make_async_copy(ob.at[z], shrink_ref.at[:, block], sems.at[28])
     own.start()
+    drain(send_8.at[0 : R - 1], sems.at[30])
+    drain(send.at[0 : R - 1], sems.at[2])
+    partner(0).wait_send()
+    partner(1).wait_send()
+    drain(send_a.at[0 : R - 1], sems.at[4])
+    drain(send_b.at[0 : R - 1], sems.at[6])
+    drain(send_9.at[0 : R - 1], sems.at[32])
+    drain(hz.at[0 : Z - 1, :, 0:32], sems.at[8])
+    drain(hp.at[0, 0 : Z - 1], sems.at[10])
+    drain(hz.at[0 : Z - 1, :, 0:32], sems.at[12])
+    drain(hp.at[0, 0 : Z - 1], sems.at[14])
+
+    @pl.when(p > 0)
+    def _():
+        above.wait_send()
+
+    @pl.when(p < R - 1)
+    def _():
+        below.wait_send()
+
+    drain(mx_r.at[0 : R - 1], sems.at[22])
+    drain(mx_z.at[0 : Z - 1], sems.at[20])
     drain(ob.at[0 : Z - 1], sems.at[25])
     drain(ob.at[0 : Z - 1], sems.at[24])
     own.wait()
@@ -678,12 +710,16 @@
         (2048, 64),
         (640, 256),
         (R, TILES, 8, 128),
-        (R, TILES + 1, 8, 128),
+        (R, TILES, 8, 128),
+        (R, 4, 128),
+        (R, 4, 128),
         (3, 256, 256),
-        (R, 3, 8, 128),
-        (R, 3, 8, 128),
-        (R, 3, 8, 128),
         (R, 2, 8, 128),
+        (R, 2, 8, 128),
+        (R, 2, 8, 128),
+        (R, 2, 8, 128),
+        (R, 4, 128),
+        (R, 4, 128),
         (Z, 4, 64, 128),
         (Z, 64, 128),
         (2, Z, 16, 128),
@@ -711,7 +747,7 @@
         out_specs=(anywhere, anywhere),
         scratch_shapes=[pltpu.VMEM(a.shape, a.dtype) for a in arguments]
         + [pltpu.VMEM(shape, F32) for shape in shapes]
-        + [dma((len(arguments),)), dma((30,))],
+        + [dma((len(arguments),)), dma((34,))],
         compiler_params=pltpu.CompilerParams(
             collective_id=0, has_side_effects=True, vmem_limit_bytes=VMEM_LIMIT
         ),

time: 66.1 us -> 65.5 us (level)
  no operation moved by 1% of the time
where the time goes in v6:
time: 65.5 us; the launch traced here: 65.4 us
  Pallas kernels  62.4 us (95%)
  other arithmetic  2.3 us (4%)
  between operations  0.67 us (1%)
    pallas_call x1, Pallas kernels, shards(): pl.pallas_call(kernel, out_shape=(block, block), in_specs=[anywhere] * le...  62.4 us
    broadcast_in_dim x1, other arithmetic, shards(): return (new[None], residual[None])  2.3 us

profile of v6, /device:TPU:1, one launch (start us, length us, event | category | flops | bytes accessed | tf_op | source)
XLA Modules:
  0.0 65.4 jit_solution(6242248016410380238)
XLA Ops:
  0.6 0.0 copy-start
  0.6 0.0 copy-start.1
  0.6 62.4 %shard_map.113 = (f32[64,2048]{1,0:T(8,128)}, f32[64,2048]{1,0:T(8,128)}) custom-call(f32[64,2048]{1,0:T(8,128)} %bitcast.12, f32[64,2048]{1,0:T(8,128)} %bitcast.13, f32[64,2048]{1,0:T(8,128)} %bitcast.14, bf16[2,256,128]{2,1,0:T(8,128)(2,1)} %constant.16.clone.real_table_in, bf16[2,256,256]{2,1,0:T(8,128)(2,1)} %constant.17.clone.row_table_in, ...), custom_call_target="tpu_custom_call" | custom-call | tf_op jit(solution)/shard_map/pallas_call | solution.py:743
  63.0 0.0 copy-done
  63.1 0.0 copy-done.1
  63.1 2.3 %subtract_bitcast_fusion.1 = (f32[1,64,2048]{2,1,0:T(8,128)}, f32[1,64,2048]{2,1,0:T(8,128)}) fusion(f32[64,2048]{1,0:T(8,128)} %get-tuple-element.4, f32[1,64,2048]{2,1,0:T(8,128)S(1)} %copy-done.1, f32[64,2048]{1,0:T(8,128)} %get-tuple-element.5, f32[1,64,2048]{2,1,0:T(8,128)S(1)} %copy-done), kind=kLoop, calls=%fused_computation.1 | loop fusion | flops 524288 | bytes 3145728 | tf_op jit(solution)/shard_map/broadcast_in_dim | solution.py:757
Async XLA Ops:
  0.6 62.4 %copy-start = (f32[1,64,2048]{2,1,0:T(8,128)S(1)}, f32[1,64,2048]{2,1,0:T(8,128)}, u32[]{:S(2)}) copy-start(f32[1,64,2048]{2,1,0:T(8,128)} %param.10) | copy-start | bytes 1572868
  0.6 62.4 %copy-start.1 = (f32[1,64,2048]{2,1,0:T(8,128)S(1)}, f32[1,64,2048]{2,1,0:T(8,128)}, u32[]{:S(2)}) copy-start(f32[1,64,2048]{2,1,0:T(8,128)} %param.11) | copy-start | bytes 1572868
